TPU v7x, 256 devices: a whole 4x4x8 slice. The times are simulated.
256 devices in a mesh: chain: 64 (over y, z, core), sub: 4 (over x).
Axes of the slice: x: 4, y: 4, z: 8, core: 2. Of those that a mesh axis runs over, the one named last changes fastest.
Arguments:
- rhs: float32 [1536, 5, 8, 512], P('chain', None, None, 'sub'), may hold values from -100 to 100
- diag_block: float32 [1536, 5, 5, 512], P('chain', None, None, 'sub')
- diag_inverse: float32 [1536, 5, 5, 512], P('chain', None, None, 'sub'), as said below
- lower_coef: float32 [1536, 2, 5, 5, 512], P('chain', None, None, None, 'sub')
- upper_coef: float32 [1536, 2, 5, 5, 512], P('chain', None, None, None, 'sub')
- side_coef: float32 [1536, 2, 5, 5, 512], P('chain', None, None, None, 'sub')
- lower_cols: int32 [1536, 2], P('chain'), may hold values from -3 to 1534, as said below
- upper_cols: int32 [1536, 2], P('chain'), may hold values from 1 to 1538, as said below
- counts: int32 [1536, 2], P('chain'), may hold values from 1 to 2
Outputs:
- correction: float32 [1536, 5, 8, 512], P('chain', None, None, 'sub')
- residual_unit: float32 [1536, 5, 8, 512], P('chain', None, None, 'sub')
Inputs may be any that keep to these rules, and one draw needn't show every extreme that they name: lower_cols[b, k] = b - d with d from 1 to 3, the two slots of a block differ, and some block has d = 3. upper_cols[b, k] = b + d with d from 1 to 3, the two slots of a block differ, and some block has d = 3. diag_inverse is the inverse of diag_block at every block and cell.
All inputs are finite; a program needn't handle non-finite values.
Results may differ from a plain program's by a relative error of at most 0.0003.
Values sent between devices are 32-bit elements; how exact they have to be, the bound alone decides.
A program may use at most 128 MiB of HBM per device.

v0:
```python
import jax
import jax.numpy as jnp
from jax import lax
from jax.sharding import Mesh
from jax.sharding import PartitionSpec as P

VARS = 5
REACH = 3
SLOTS = 2
CHAIN = ("chain_0", "chain_1", "chain_2")
CHAIN_SUB = ("chain_0", "chain_1", "chain_2", "sub")


def filled_with(x, identity):
    return jax.tree.map(
        lambda a, e: jnp.broadcast_to(jnp.asarray(e, a.dtype), a.shape), x, identity
    )


def prefix_by_axis(x, axes, combine, identity, reverse):
    before = start = filled_with(x, identity)
    so_far = x
    for axis in reversed(axes):
        count, index = (lax.axis_size(axis), lax.axis_index(axis))
        pieces = jax.tree.map(lambda part: lax.all_gather(part, axis), so_far)
        inside, so_far = (start, start)
        for k in reversed(range(count)) if reverse else range(count):
            passed = k > index if reverse else k < index
            so_far = combine(so_far, jax.tree.map(lambda part: part[k], pieces))
            inside = jax.tree.map(lambda new, old: jnp.where(passed, new, old), so_far, inside)
        before = combine(inside, before)
    return before


def extended_2(cells, sides, width):
    for axis, dim in sides:
        count = lax.axis_size(axis)
        ends = count - 1
        head = lax.slice_in_dim(cells, 0, width, axis=dim)
        tail = lax.slice_in_dim(cells, cells.shape[dim] - width, cells.shape[dim], axis=dim)
        cells = jnp.concatenate(
            [
                lax.ppermute(tail, axis, [(i, (i + 1) % count) for i in range(ends)]),
                cells,
                lax.ppermute(head, axis, [((i + 1) % count, i) for i in range(ends)]),
            ],
            axis=dim,
        )
    return cells


def over_axes(x, axes):
    for axis in axes:
        x = lax.psum(x, axis)
    return x


def block_apply_matrix(matrix, vector):
    total = matrix[:, 0, None, :] * vector[0][None]
    for inner in range(1, VARS):
        total = total + matrix[:, inner, None, :] * vector[inner][None]
    return total


def apply_many(matrix, vector):
    total = matrix[:, :, 0, None, :] * vector[:, 0][:, None]
    for inner in range(1, VARS):
        total = total + matrix[:, :, inner, None, :] * vector[:, inner][:, None]
    return total


def compose(earlier, later):
    g_early, p_early = earlier
    g_late, late_partial = later
    high = lax.Precision.HIGHEST
    g_new = jnp.einsum("...ijc,...jqc->...iqc", g_late, g_early, precision=high)
    p_new = jnp.einsum("...ijc,...jqc->...iqc", g_late, p_early, precision=high) + late_partial
    return (g_new, p_new)


def sweep(coef, inverse, source, offsets, active, start, forward):

    def step(window, item):
        mats, inv, src, off, act = item
        acc = jnp.zeros_like(src)
        for slot in range(SLOTS):
            pick = (jnp.arange(REACH, dtype=jnp.int32) == off[slot] - 1).astype(jnp.float32)
            near = jnp.sum(pick[:, None, None, None] * window, axis=0)
            acc = acc + act[slot] * block_apply_matrix(mats[slot], near)
        if forward:
            out = block_apply_matrix(inv, src - acc)
        else:
            out = src - block_apply_matrix(inv, acc)
        return (jnp.concatenate([out[None], window[:-1]], 0), out)

    unused, outs = lax.scan(
        step, start, (coef, inverse, source, offsets, active), reverse=not forward, unroll=4
    )
    return outs


def entering(maps_g, maps_p, forward):
    cells = maps_g.shape[2]
    width = maps_g.shape[0]
    ident = (
        jnp.eye(width, dtype=jnp.float32)[:, :, None] * jnp.ones((1, 1, cells), jnp.float32),
        jnp.zeros_like(maps_p),
    )
    if forward:
        g_in, p_in = prefix_by_axis((maps_g, maps_p), CHAIN, compose, ident, False)
    else:
        g_in, p_in = prefix_by_axis((maps_g, maps_p), CHAIN, compose, ident, True)
    return p_in


def solve_side(coef, inverse, source, offsets, active, forward):
    blocks, nvars, width_rhs, cells = source.shape
    width = REACH * VARS
    basis = (jnp.arange(width)[:, None] == jnp.arange(width)[None, :]).astype(jnp.float32)
    basis = basis.reshape(REACH, VARS, width)[:, :, :, None] * jnp.ones(
        (1, 1, 1, cells), jnp.float32
    )
    start = jnp.concatenate([jnp.zeros((REACH, VARS, width_rhs, cells), jnp.float32), basis], 2)
    padded = jnp.concatenate([source, jnp.zeros((blocks, VARS, width, cells), jnp.float32)], 2)
    first_pass = sweep(coef, inverse, padded, offsets, active, start, forward)
    if forward:
        edge = jnp.flip(first_pass[blocks - REACH :], 0)
    else:
        edge = first_pass[:REACH]
    edge = edge.reshape(width, width_rhs + width, cells)
    p_in = entering(edge[:, width_rhs:], edge[:, :width_rhs], forward)
    response = first_pass[:, :, width_rhs:]
    result = first_pass[:, :, :width_rhs] + jnp.einsum(
        "bvqc,qrc->bvrc", response, p_in, precision=lax.Precision.HIGHEST
    )
    return (result, p_in)


def shards(
    rhs, diag_block, diag_inverse, lower_coef, upper_coef, side_coef, lower_cols, upper_cols, counts
):
    blocks, nvars, width_rhs, cells = rhs.shape
    rows = lax.axis_index(CHAIN) * blocks + jnp.arange(blocks, dtype=jnp.int32)
    slot_ids = jnp.arange(SLOTS, dtype=jnp.int32)
    lower_off = rows[:, None] - lower_cols
    upper_off = upper_cols - rows[:, None]
    act_low = (slot_ids[None, :] < counts[:, 0:1]).astype(jnp.float32)
    act_up = (slot_ids[None, :] < counts[:, 1:2]).astype(jnp.float32)
    ysweep, unused = solve_side(lower_coef, diag_inverse, rhs, lower_off, act_low, True)
    correction, head_in = solve_side(upper_coef, diag_inverse, ysweep, upper_off, act_up, False)
    extended = extended_2(correction, ((CHAIN, 0),), REACH)
    image = apply_many(diag_block, correction)
    local_rows = jnp.arange(blocks, dtype=jnp.int32)
    for slot in range(SLOTS):
        near = jnp.take(extended, REACH + local_rows - lower_off[:, slot], axis=0)
        image = image + act_low[:, slot, None, None, None] * apply_many(lower_coef[:, slot], near)
        near = jnp.take(extended, REACH + local_rows + upper_off[:, slot], axis=0)
        image = image + act_up[:, slot, None, None, None] * apply_many(upper_coef[:, slot], near)
    widened = extended_2(correction, (("sub", 3),), 1)
    image = image + apply_many(side_coef[:, 0], widened[..., :cells])
    image = image + apply_many(side_coef[:, 1], widened[..., 2:])
    resid = rhs - image
    partial_sq = jnp.sum(resid * resid, axis=(0, 1, 3))
    total_sq = over_axes(partial_sq, CHAIN_SUB)
    entries = blocks * VARS * cells * lax.axis_size(CHAIN) * lax.axis_size("sub")
    msq = total_sq / entries
    residual_unit = resid * lax.rsqrt(msq + 1e-06)[None, None, :, None]
    return (correction, residual_unit)


def solution(mesh):
    split = Mesh(
        mesh.devices.reshape(4, 8, 2, mesh.shape["sub"]), ("chain_0", "chain_1", "chain_2", "sub")
    )
    placed = (
        P(CHAIN, None, None, "sub"),
        P(CHAIN, None, None, "sub"),
        P(CHAIN, None, None, "sub"),
        P(CHAIN, None, None, None, "sub"),
        P(CHAIN, None, None, None, "sub"),
        P(CHAIN, None, None, None, "sub"),
        P(CHAIN, None),
        P(CHAIN, None),
        P(CHAIN, None),
    )
    return jax.shard_map(
        shards,
        mesh=split,
        in_specs=placed,
        out_specs=(P(CHAIN, None, None, "sub"), P(CHAIN, None, None, "sub")),
        check_vma=False,
    )
```

profile of v0, /device:TPU:1, one launch (start us, length us, event | category | flops | bytes accessed | tf_op | source)
XLA Modules:
  0.0 710.3 jit_solution(4729624152276036764)
XLA Ops:
  6.8 85.5 %while.32 = (s32[]{:T(128)}, f32[3,5,23,128]{3,2,1,0:T(8,128)S(1)}, f32[6,4,5,23,128]{4,1,0,3,2:T(4,128)S(1)}, f32[6,4,5,5,128]{4,2,3,1,0:T(8,128)}, f32[6,4,5,2...) while((s32[]{:T(128)}, f32[3,5,23,128]{3,2,1,0:T(8,128)S(1)}, ...), condition=%wide.region_9.10_spmd, body=%wide.region_0.9_spmd.sunk | while | flops 2855741 | bytes 7196913 | solution.py:96
  93.7 4.8 all-gather
  113.8 21.6 %all-gather.4 = f32[120,8,128]{2,1,0:T(8,128)S(1)} all-gather(f32[15,8,128]{2,1,0:T(8,128)S(1)} %copy.300), channel_id=6, replica_groups=mesh['chain_0'=4,'chain_1'=8,'chain_2'=2,'sub'=4] {'chain_1'}, dimensions={0}, use_global_device_ids=true | all-gather | bytes 552960 | tf_op jit(solution)/shard_map/all_gather | solution.py:25
  144.3 21.5 %all-gather.1 = f32[120,15,128]{2,1,0:T(8,128)S(1)} all-gather(f32[15,15,128]{2,1,0:T(8,128)S(1)} %copy.287), channel_id=3, replica_groups=mesh['chain_0'=4,'chain_1'=8,'chain_2'=2,'sub'=4] {'chain_1'}, dimensions={0}, use_global_device_ids=true | all-gather | bytes 1036800 | tf_op jit(solution)/shard_map/all_gather | solution.py:25
  170.8 3.6 fusion.44
  237.9 9.8 %all-gather.5 = f32[60,8,128]{2,1,0:T(8,128)S(1)} all-gather(f32[15,8,128]{2,1,0:T(8,128)S(1)} %copy.309), channel_id=7, replica_groups=mesh['chain_0'=4,'chain_1'=8,'chain_2'=2,'sub'=4] {'chain_0'}, dimensions={0}, use_global_device_ids=true | all-gather | bytes 307200 | tf_op jit(solution)/shard_map/all_gather | solution.py:25
  254.2 10.8 %all-gather.2 = f32[60,15,128]{2,1,0:T(8,128)S(1)} all-gather(f32[15,15,128]{2,1,0:T(8,128)S(1)} %copy.296), channel_id=4, replica_groups=mesh['chain_0'=4,'chain_1'=8,'chain_2'=2,'sub'=4] {'chain_0'}, dimensions={0}, use_global_device_ids=true | all-gather | bytes 576000 | tf_op jit(solution)/shard_map/all_gather | solution.py:25
  274.2 4.1 copy.453
  290.8 4.8 bitcast_add_fusion.1
  299.7 87.4 %while.33 = (s32[]{:T(128)}, f32[3,5,23,128]{3,2,1,0:T(8,128)S(1)}, f32[6,4,5,23,128]{4,1,0,3,2:T(4,128)S(1)}, f32[6,4,5,23,128]{4,1,0,3,2:T(4,128)S(1)}, f32[6,...) while((s32[]{:T(128)}, f32[3,5,23,128]{3,2,1,0:T(8,128)S(1)}, ...), condition=%wide.region_19.20_spmd, body=%wide.region_10.19_spmd.sunk | while | flops 2855742 | bytes 7667961 | solution.py:96
  388.1 17.8 %all-gather.6 = f32[30,15,128]{2,1,0:T(8,128)S(1)} all-gather(f32[15,15,128]{2,1,0:T(8,128)S(1)} %slice.3801), channel_id=8, replica_groups=mesh['chain_0'=4,'chain_1'=8,'chain_2'=2,'sub'=4] {'chain_2'}, dimensions={0}, use_global_device_ids=true | all-gather | bytes 345600 | tf_op jit(solution)/shard_map/all_gather | solution.py:25
  421.2 20.2 %all-gather.10 = f32[120,8,128]{2,1,0:T(8,128)S(1)} all-gather(f32[15,8,128]{2,1,0:T(8,128)S(1)} %copy.346), channel_id=12, replica_groups=mesh['chain_0'=4,'chain_1'=8,'chain_2'=2,'sub'=4] {'chain_1'}, dimensions={0}, use_global_device_ids=true | all-gather | bytes 552960 | tf_op jit(solution)/shard_map/all_gather | solution.py:25
  450.1 20.3 %all-gather.7 = f32[120,15,128]{2,1,0:T(8,128)S(1)} all-gather(f32[15,15,128]{2,1,0:T(8,128)S(1)} %copy.333), channel_id=9, replica_groups=mesh['chain_0'=4,'chain_1'=8,'chain_2'=2,'sub'=4] {'chain_1'}, dimensions={0}, use_global_device_ids=true | all-gather | bytes 1036800 | tf_op jit(solution)/shard_map/all_gather | solution.py:25
  475.5 3.6 fusion.29
  541.3 9.3 %all-gather.11 = f32[60,8,128]{2,1,0:T(8,128)S(1)} all-gather(f32[15,8,128]{2,1,0:T(8,128)S(1)} %copy.355), channel_id=13, replica_groups=mesh['chain_0'=4,'chain_1'=8,'chain_2'=2,'sub'=4] {'chain_0'}, dimensions={0}, use_global_device_ids=true | all-gather | bytes 307200 | tf_op jit(solution)/shard_map/all_gather | solution.py:25
  554.8 10.9 %all-gather.8 = f32[60,15,128]{2,1,0:T(8,128)S(1)} all-gather(f32[15,15,128]{2,1,0:T(8,128)S(1)} %copy.342), channel_id=10, replica_groups=mesh['chain_0'=4,'chain_1'=8,'chain_2'=2,'sub'=4] {'chain_0'}, dimensions={0}, use_global_device_ids=true | all-gather | bytes 576000 | tf_op jit(solution)/shard_map/all_gather | solution.py:25
  568.7 4.1 copy.465
  588.6 4.2 collective-permute-start.2
  599.0 19.9 %collective-permute-start.1 = (f32[3,5,8,128]{3,2,1,0:T(8,128)}, f32[3,5,8,128]{3,2,1,0:T(8,128)}, u32[]{:S(2)}, u32[]{:S(2)}) collective-permute-start(f32[3,5,8,128]{3,2,1,0:T(8,128)} %copy.382), channel_id=1, source_target_pairs={{4,0},{8,4},{12,8},{16,12},{20,16},{24,20},{28,24},{32,28},{36,32}... | collective-permute-start | bytes 184328 | tf_op jit(solution)/shard_map/ppermute | solution.py:45
  667.0 6.0 multiply_reduce_fusion.16
  673.0 8.4 %psum.28 = f32[8]{0:T(128)S(1)} all-reduce(f32[8]{0:T(128)S(1)} %get-tuple-element.427), channel_id=1, replica_groups=mesh['chain_0'=4,'chain_1'=8,'chain_2'=2,'sub'=4] {'chain_0'}, use_global_device_ids=true, to_apply=%region_21.23 | all-reduce | flops 8 | bytes 64 | tf_op jit(solution)/shard_map/psum | solution.py:54
  681.4 11.1 %psum.29 = f32[8]{0:T(128)S(1)} all-reduce(f32[8]{0:T(128)S(1)} %psum.28), channel_id=1, replica_groups=mesh['chain_0'=4,'chain_1'=8,'chain_2'=2,'sub'=4] {'chain_1'}, use_global_device_ids=true, to_apply=%region_22.24 | all-reduce | flops 8 | bytes 64 | tf_op jit(solution)/shard_map/psum | solution.py:54
  692.5 8.9 %psum.30 = f32[8]{0:T(128)S(1)} all-reduce(f32[8]{0:T(128)S(1)} %psum.29), channel_id=1, replica_groups=mesh['chain_0'=4,'chain_1'=8,'chain_2'=2,'sub'=4] {'chain_2'}, use_global_device_ids=true, to_apply=%region_23.25 | all-reduce | flops 8 | bytes 64 | tf_op jit(solution)/shard_map/psum | solution.py:54
  701.4 7.5 %psum.31 = f32[8]{0:T(128)S(1)} all-reduce(f32[8]{0:T(128)S(1)} %psum.30), channel_id=1, replica_groups=mesh['chain_0'=4,'chain_1'=8,'chain_2'=2,'sub'=4] {'sub'}, use_global_device_ids=true, to_apply=%region_24.26 | all-reduce | flops 8 | bytes 64 | tf_op jit(solution)/shard_map/psum | solution.py:54
  (1067 shorter events, 410.6 us)
Async XLA Ops:
  0.6 5.8 copy-start.120
  0.6 5.9 copy-start.101
  92.4 6.2 copy-start.52
  188.9 6.2 copy-start.3
  188.9 6.2 copy-start.91
  278.3 6.5 copy-start.95
  278.3 12.5 %slice-start = ((s8[5242880]{0:T(1024)(128)(4,1)}), s8[4194304]{0:T(1024)(128)(4,1)S(1)}, s32[]{:S(2)}) async-start(s8[5242880]{0:T(1024)(128)(4,1)} %bitcast.1279), calls=%async_computation | async-start | bytes 8388608
  281.5 6.4 copy-start.75
  284.8 6.0 slice-start.1
  387.1 18.9 %copy-start.50 = (f32[6,4,5,23,128]{4,1,0,3,2:T(4,128)}, f32[6,4,5,23,128]{4,1,0,3,2:T(4,128)S(1)}, u32[]{:S(2)}) copy-start(f32[6,4,5,23,128]{4,1,0,3,2:T(4,128)S(1)} %get-tuple-element.322) | copy-start | bytes 4239364
  492.7 6.2 copy-start.15
  492.7 6.2 copy-start.93
  572.8 6.1 copy-start.96
  572.8 10.7 %slice-start.2 = ((s8[5242880]{0:T(1024)(128)(4,1)}), s8[4194304]{0:T(1024)(128)(4,1)S(1)}, s32[]{:S(2)}) async-start(s8[5242880]{0:T(1024)(128)(4,1)} %bitcast.1281), calls=%async_computation.2 | async-start | bytes 8388608
  587.3 70.8 %collective-permute-start.3 = (f32[24,5,8,1]{0,2,1,3:T(8,128)}, f32[24,5,8,1]{0,2,1,3:T(8,128)}, u32[]{:S(2)}, u32[]{:S(2)}) collective-permute-start(f32[24,5,8,1]{0,2,1,3:T(8,128)} %get-tuple-element.827), channel_id=1, source_target_pairs={{1,0},{2,1},{3,2},{5,4},{6,5},{7,6},{9,8},{10,9},{11,10},{13,12},{... | collective-permute-start | bytes 11528 | tf_op jit(solution)/shard_map/ppermute | solution.py:45
  588.6 70.9 %collective-permute-start.2 = (f32[24,5,8,1]{0,2,1,3:T(8,128)}, f32[24,5,8,1]{0,2,1,3:T(8,128)S(1)}, u32[]{:S(2)}, u32[]{:S(2)}) collective-permute-start(f32[24,5,8,1]{0,2,1,3:T(8,128)} %get-tuple-element.826), channel_id=1, source_target_pairs={{0,1},{1,2},{2,3},{4,5},{5,6},{6,7},{8,9},{9,10},{10,11},{12,13},{... | collective-permute-start | bytes 11528 | tf_op jit(solution)/shard_map/ppermute | solution.py:43
  599.0 61.5 %collective-permute-start.1 = (f32[3,5,8,128]{3,2,1,0:T(8,128)}, f32[3,5,8,128]{3,2,1,0:T(8,128)}, u32[]{:S(2)}, u32[]{:S(2)}) collective-permute-start(f32[3,5,8,128]{3,2,1,0:T(8,128)} %copy.382), channel_id=1, source_target_pairs={{4,0},{8,4},{12,8},{16,12},{20,16},{24,20},{28,24},{32,28},{36,32}... | collective-permute-start | bytes 184328 | tf_op jit(solution)/shard_map/ppermute | solution.py:45
  622.1 38.4 %collective-permute-start = (f32[3,5,8,128]{3,2,1,0:T(8,128)}, f32[3,5,8,128]{3,2,1,0:T(8,128)}, u32[]{:S(2)}, u32[]{:S(2)}) collective-permute-start(f32[3,5,8,128]{3,2,1,0:T(8,128)} %copy.381), channel_id=1, source_target_pairs={{0,4},{4,8},{8,12},{12,16},{16,20},{20,24},{24,28},{28,32},{32,36}... | collective-permute-start | bytes 184328 | tf_op jit(solution)/shard_map/ppermute | solution.py:43
  626.0 34.6 %copy-start.49 = (f32[24,5,8,128]{3,2,1,0:T(8,128)}, f32[24,5,8,128]{3,2,1,0:T(8,128)S(1)}, u32[]{:S(2)}) copy-start(f32[24,5,8,128]{3,2,1,0:T(8,128)S(1)} %copy.422) | copy-start | bytes 1474564
  634.6 19.0 %copy-start.83 = (f32[24,8,128]{0,1,2:T(8,128)S(1)}, f32[24,8,128]{0,1,2:T(8,128)}, u32[]{:S(2)}) copy-start(f32[24,8,128]{0,1,2:T(8,128)} %get-tuple-element.820) | copy-start | bytes 294916
  635.3 19.2 %copy-start.82 = (f32[24,8,128]{0,1,2:T(8,128)S(1)}, f32[24,8,128]{0,1,2:T(8,128)}, u32[]{:S(2)}) copy-start(f32[24,8,128]{0,1,2:T(8,128)} %get-tuple-element.821) | copy-start | bytes 294916
  638.6 16.8 %copy-start.81 = (f32[24,8,128]{0,1,2:T(8,128)S(1)}, f32[24,8,128]{0,1,2:T(8,128)}, u32[]{:S(2)}) copy-start(f32[24,8,128]{0,1,2:T(8,128)} %get-tuple-element.822) | copy-start | bytes 294916
  641.9 14.4 %copy-start.80 = (f32[24,8,128]{0,1,2:T(8,128)S(1)}, f32[24,8,128]{0,1,2:T(8,128)}, u32[]{:S(2)}) copy-start(f32[24,8,128]{0,1,2:T(8,128)} %get-tuple-element.823) | copy-start | bytes 294916
  645.1 12.0 %copy-start.79 = (f32[24,8,128]{0,1,2:T(8,128)S(1)}, f32[24,8,128]{0,1,2:T(8,128)}, u32[]{:S(2)}) copy-start(f32[24,8,128]{0,1,2:T(8,128)} %get-tuple-element.819) | copy-start | bytes 294916
  (106 other events, 339.4 us)
where the time goes:
time: 724 us; the launch traced here: 710 us
  local copies, waits for them, and re-layouts  209 us (29%)
  blocking collectives  187 us (26%)
  matrix products  141 us (19%)
  other arithmetic  79.4 us (11%)
  loops' own time  62.8 us (9%)
  starting transfers between devices  28.5 us (4%)
    all_gather x12, blocking collectives, prefix_by_axis(): pieces = jax.tree.map(lambda part: lax.all_gather(part, axis), so_far)  151 us
    dot_general x34, matrix products, compose(): jnp.einsum('...ijc,...jqc->...iqc', g_late, p_early, precision=high)  83 us
    another operation x2, loops' own time, sweep(): lax.scan(step, start, (coef, inverse, source, offsets, active), reverse=n...  62.8 us
    unnamed x282, local copies, waits for them, and re-layouts  59 us
    dot_general x24, matrix products, compose(): g_new = jnp.einsum('...ijc,...jqc->...iqc', g_late, g_early, precision=high)  49.8 us
    slice x48, local copies, waits for them, and re-layouts, prefix_by_axis(): so_far = combine(so_far, jax.tree.map(lambda part: part[k], pieces))  45.6 us
    psum x4, blocking collectives, over_axes(): x = lax.psum(x, axis)  36 us
    add x24, other arithmetic, step(): acc = acc + act[slot] * block_apply_matrix(mats[slot], near)  31 us
  transfers between devices with their start and end apart: 4, of which 0 were waited for; matrix products, arithmetic and copies ran while one was open for 6% of the time, Pallas kernels for 0%

commit v1 on v0

v1 whole, which is shorter than its diff:
```python
import functools

import jax
import jax.numpy as jnp
from jax import lax
from jax.experimental import pallas as pl
from jax.experimental.pallas import tpu as pltpu
from jax.sharding import PartitionSpec as P

VARS = 5
RHS = 8
REACH = 3
SLOTS = 2
STATE = REACH * VARS
LANES = 128
PAIR = VARS * VARS * SLOTS
FWIDE = 24
BWIDE = 40
FROWS = STATE * FWIDE
OUT_TILES = 8
BACK_TILES = 2
F32 = jnp.float32
VMEM = pltpu.VMEM
MESH = pl.DeviceIdType.MESH


def row(ref, *index):
    *lead, at = index
    return ref[(*lead, pl.ds(at, RHS, stride=0), slice(None))]


def lanes_of(shape):
    return lax.broadcasted_iota(jnp.int32, shape, len(shape) - 1)


def chunk(t):
    return slice(8 * t, 8 * t + 8)


def near(cols, counts, side, slot, b, start, forward, absent):
    col = cols[slot, b] - start
    used = slot < counts[side, b]
    return jnp.where(used, col + REACH if forward else col, absent)


def local_kernel(blocks, lcol, ucol, counts, rhs, dinv, low, up, send, z, aup, alow, y, vals):
    start = lax.axis_index("chain") * blocks
    absent = blocks + REACH

    for coef, out in ((low, alow), (up, aup)):
        for group in range(blocks // 8):
            rows = pl.ds(8 * group, 8)
            inv = [dinv[q, rows, :] for q in range(VARS * VARS)]
            for slot in range(SLOTS):
                for j in range(VARS):
                    col = [
                        coef[pl.ds(8 * group * PAIR + (m * VARS + j) * SLOTS + slot, 8, stride=PAIR), :]
                        for m in range(VARS)
                    ]
                    for i in range(VARS):
                        acc = inv[i * VARS] * col[0]
                        for m in range(1, VARS):
                            acc = acc + inv[i * VARS + m] * col[m]
                        out[slot * 25 + i * VARS + j, rows, :] = acc

    fsub = lax.broadcasted_iota(jnp.int32, (FWIDE, LANES), 0)
    bsub = lax.broadcasted_iota(jnp.int32, (BWIDE, LANES), 0)
    for d in range(1, REACH + 1):
        for v in range(VARS):
            q = (d - 1) * VARS + v
            y[REACH - d, v] = jnp.where(fsub == RHS + q, 1.0, 0.0).astype(F32)
            z[blocks - 1 + d, v] = jnp.where(bsub == FWIDE + q, 1.0, 0.0).astype(F32)
    for v in range(VARS):
        y[absent, v] = jnp.zeros((FWIDE, LANES), F32)
        z[absent, v] = jnp.zeros((BWIDE, LANES), F32)

    def forward(b, carry):
        at = [near(lcol, counts, 0, k, b, start, True, absent) for k in range(SLOTS)]
        e = [
            [[y[at[k], j, chunk(t), :] for t in range(3)] for j in range(VARS)]
            for k in range(SLOTS)
        ]
        src = [rhs[b, m] for m in range(VARS)]
        for i in range(VARS):
            w = row(dinv, i * VARS, b) * src[0]
            for m in range(1, VARS):
                w = w + row(dinv, i * VARS + m, b) * src[m]
            part = []
            for k in range(SLOTS):
                acc = None
                for j in range(VARS):
                    c = row(alow, k * 25 + i * VARS + j, b)
                    new = [c * e[k][j][t] for t in range(3)]
                    acc = new if acc is None else [p + q for p, q in zip(acc, new)]
                part.append(acc)
            for t in range(3):
                total = part[0][t] + part[1][t]
                y[b + REACH, i, chunk(t), :] = w - total if t == 0 else -total
        return carry

    lax.fori_loop(0, blocks, forward, 0)

    def backward(step, carry):
        b = blocks - 1 - step
        at = [near(ucol, counts, 1, k, b, start, False, absent) for k in range(SLOTS)]
        for group in ((0, 1, 2), (3, 4)):
            e = [
                [[z[at[k], j, chunk(t), :] for t in group] for j in range(VARS)]
                for k in range(SLOTS)
            ]
            for i in range(VARS):
                part = []
                for k in range(SLOTS):
                    acc = None
                    for j in range(VARS):
                        c = row(aup, k * 25 + i * VARS + j, b)
                        new = [c * x for x in e[k][j]]
                        acc = new if acc is None else [p + q for p, q in zip(acc, new)]
                    part.append(acc)
                for n, t in enumerate(group):
                    total = part[0][n] + part[1][n]
                    z[b, i, chunk(t), :] = y[b + REACH, i, chunk(t), :] - total if t < 3 else -total
        return carry

    lax.fori_loop(0, blocks, backward, 0)

    for d in range(1, REACH + 1):
        for v in range(VARS):
            q = (d - 1) * VARS + v
            vals[q * FWIDE : (q + 1) * FWIDE, :] = y[REACH + blocks - d, v]
            vals[FROWS + q * BWIDE : FROWS + (q + 1) * BWIDE, :] = z[d - 1, v]
    used = FROWS + STATE * BWIDE
    vals[used:, :] = jnp.zeros((OUT_TILES * LANES - used, LANES), F32)
    half = LANES // 2
    for tile in range(OUT_TILES):
        turned = vals[tile * LANES : (tile + 1) * LANES, :].T
        for c in range(2):
            for first in range(0, half, 8):
                at = (first * 2 + c) * OUT_TILES + tile
                send[pl.ds(at, 8, stride=2 * OUT_TILES), :] = turned[c * half + first : c * half + first + 8]


def exchange_kernel(nodes, src, dst, send_sem, recv_sem, own_sem):
    me = lax.axis_index("chain")
    barrier = pltpu.get_barrier_semaphore()

    def greet(k, carry):
        pl.semaphore_signal(
            barrier, inc=1, device_id={"chain": lax.rem(me + k, nodes)}, device_id_type=MESH
        )
        return carry

    lax.fori_loop(1, nodes, greet, 0)
    own = pltpu.make_async_copy(src.at[me], dst.at[me], own_sem)
    own.start()
    pl.semaphore_wait(barrier, nodes - 1)

    def post(k, carry):
        to = lax.rem(me + k, nodes)
        pltpu.make_async_remote_copy(
            src_ref=src.at[to],
            dst_ref=dst.at[me],
            send_sem=send_sem,
            recv_sem=recv_sem,
            device_id={"chain": to},
            device_id_type=MESH,
        ).start()
        return carry

    lax.fori_loop(1, nodes, post, 0)
    own.wait()
    pltpu.make_async_remote_copy(
        src_ref=src.at[pl.ds(0, nodes - 1)],
        dst_ref=dst.at[pl.ds(0, nodes - 1)],
        send_sem=send_sem,
        recv_sem=recv_sem,
        device_id={"chain": lax.rem(me + 1, nodes)},
        device_id_type=MESH,
    ).wait()


def exchange(x, nodes, collective_id):
    x = x.reshape(nodes, x.shape[0] // nodes, LANES)
    out = pl.pallas_call(
        functools.partial(exchange_kernel, nodes),
        out_shape=jax.ShapeDtypeStruct(x.shape, x.dtype),
        in_specs=[pl.BlockSpec(memory_space=pl.ANY)],
        out_specs=pl.BlockSpec(memory_space=pl.ANY),
        scratch_shapes=[pltpu.SemaphoreType.DMA] * 3,
        compiler_params=pltpu.CompilerParams(collective_id=collective_id, has_side_effects=True),
        name=f"exchange{collective_id}",
    )(x)
    return out.reshape(x.shape[0] * x.shape[1], LANES)


def scan(read, write, lane, span, ahead):
    shift = 1
    while shift < span:
        last = 2 * shift >= span
        turn = LANES - shift if ahead else shift
        inside = lane < span - shift if ahead else lane >= shift
        old = [[read(i, t) for t in range(3)] for i in range(STATE)]
        new = []
        for t in range(1 if last else 3):
            e = [pltpu.roll(old[j][t], turn, 1) for j in range(STATE)]
            fresh = []
            for i in range(STATE):
                acc = old[i][0] if t == 0 else None
                for j in range(STATE):
                    term = write.coef(i, j) * e[j]
                    acc = term if acc is None else acc + term
                fresh.append(jnp.where(inside, acc, old[i][t]))
            new.append(fresh)
        write.store(new)
        shift *= 2


class Maps:
    def __init__(self, front, back):
        self.front, self.back = front, back

    def read(self, i, t):
        return self.front[i, chunk(t), :]

    def coef(self, i, j):
        return row(self.front, i, RHS + j)

    def store(self, new):
        for t, column in enumerate(new):
            for i, value in enumerate(column):
                self.back[i, chunk(t), :] = value
        self.front, self.back = self.back, self.front


def chain_kernel(nodes, recv, back, vals, m0, m1):
    half = LANES // 2
    for tile in range(OUT_TILES):
        both = [recv[pl.ds(c * OUT_TILES + tile, half, stride=2 * OUT_TILES), :] for c in range(2)]
        vals[tile * LANES : (tile + 1) * LANES, :] = jnp.concatenate(both, 0).T
    lane = lax.rem(lanes_of((8, LANES)), nodes)

    for i in range(STATE):
        m0[i] = vals[i * FWIDE : (i + 1) * FWIDE, :]
    maps = Maps(m0, m1)
    scan(maps.read, maps, lane, nodes, False)
    entering = [
        jnp.where(lane == 0, 0.0, pltpu.roll(maps.read(i, 0), 1, 1)) for i in range(STATE)
    ]

    for i in range(STATE):
        at = FROWS + i * BWIDE
        acc = vals[at : at + 8, :]
        for j in range(STATE):
            acc = acc + row(vals, at + RHS + j) * entering[j]
        m0[i, chunk(0), :] = acc
        m0[i, 8:24, :] = vals[at + FWIDE : at + BWIDE, :]
    maps = Maps(m0, m1)
    scan(maps.read, maps, lane, nodes, True)
    following = [
        jnp.where(lane == nodes - 1, 0.0, pltpu.roll(maps.read(i, 0), LANES - 1, 1))
        for i in range(STATE)
    ]

    for tile, state in enumerate((entering, following)):
        turned = jnp.concatenate(state + [jnp.zeros((8, LANES), F32)], 0).T
        for c in range(2):
            for first in range(0, half, 8):
                at = (first * 2 + c) * BACK_TILES + tile
                back[pl.ds(at, 8, stride=2 * BACK_TILES), :] = turned[c * half + first : c * half + first + 8]


def correct_kernel(blocks, ucol, counts, back, z, aup, corr, u, edges, padded):
    start = lax.axis_index("chain") * blocks
    absent = blocks + REACH
    half = LANES // 2
    state = []
    for tile in range(BACK_TILES):
        both = [back[pl.ds(c * BACK_TILES + tile, half, stride=2 * BACK_TILES), :] for c in range(2)]
        turned = jnp.concatenate(both, 0).T
        state.append([turned[8 * q : 8 * q + 8] for q in range(STATE)])
    entering, following = state
    for d in range(1, REACH + 1):
        for v in range(VARS):
            padded[blocks - 1 + d, v] = following[(d - 1) * VARS + v]
    for v in range(VARS):
        padded[absent, v] = jnp.zeros((RHS, LANES), F32)
    lane = lanes_of((RHS, LANES))

    def solve(b, carry):
        head, tail = carry
        for i in range(VARS):
            acc = [z[b, i, chunk(0), :], None]
            for n, (offset, values) in enumerate(((RHS, entering), (FWIDE, following))):
                for j in range(STATE):
                    term = row(z, b, i, offset + j) * values[j]
                    acc[n] = term if acc[n] is None else acc[n] + term
            value = acc[0] + acc[1]
            corr[b, i] = value
            padded[b, i] = value
            here = lane == b * VARS + i
            head = jnp.where(here, value[:, 0:1], head)
            tail = jnp.where(here, value[:, LANES - 1 :], tail)
        return head, tail

    none = jnp.zeros((RHS, LANES), F32)
    head, tail = lax.fori_loop(0, blocks, solve, (none, none))
    edges[0] = head
    edges[1] = tail

    def couple(b, carry):
        at = [near(ucol, counts, 1, k, b, start, False, absent) for k in range(SLOTS)]
        e = [[padded[at[k], j] for j in range(VARS)] for k in range(SLOTS)]
        for i in range(VARS):
            part = []
            for k in range(SLOTS):
                acc = row(aup, k * 25 + i * VARS, b) * e[k][0]
                for j in range(1, VARS):
                    acc = acc + row(aup, k * 25 + i * VARS + j, b) * e[k][j]
                part.append(acc)
            u[b, i] = part[0] + part[1]
        return carry

    lax.fori_loop(0, blocks, couple, 0)


def halo_kernel(nodes, subs, blocks, u, edges, before, beside, send_sem, recv_sem):
    me, sub = lax.axis_index("chain"), lax.axis_index("sub")
    left, right = lax.rem(sub + subs - 1, subs), lax.rem(sub + 1, subs)
    later, earlier = lax.rem(me + 1, nodes), lax.rem(me + nodes - 1, nodes)
    barrier = pltpu.get_barrier_semaphore()
    for peer in ({"sub": left}, {"sub": right}, {"chain": later}, {"chain": earlier}):
        pl.semaphore_signal(barrier, inc=1, device_id=peer, device_id_type=MESH)
    pl.semaphore_wait(barrier, 4)
    plan = (
        (u.at[pl.ds(blocks - REACH, REACH)], before, {"chain": later}),
        (edges.at[1], beside.at[0], {"sub": right}),
        (edges.at[0], beside.at[1], {"sub": left}),
    )
    copies = [
        pltpu.make_async_remote_copy(
            src_ref=src,
            dst_ref=dst,
            send_sem=send_sem.at[n],
            recv_sem=recv_sem.at[n],
            device_id=peer,
            device_id_type=MESH,
        )
        for n, (src, dst, peer) in enumerate(plan)
    ]
    for copy in copies:
        copy.start()
    for copy in copies:
        copy.wait()


def resid_kernel(blocks, subs, lcol, counts, low, side, corr, u, before, beside, resid, part, padded):
    me, sub = lax.axis_index("chain"), lax.axis_index("sub")
    start = me * blocks
    absent = blocks + REACH
    for d in range(REACH):
        for v in range(VARS):
            padded[d, v] = jnp.where(me == 0, 0.0, before[d, v])
    for v in range(VARS):
        padded[absent, v] = jnp.zeros((RHS, LANES), F32)

    def fill(b, carry):
        for v in range(VARS):
            padded[b + REACH, v] = u[b, v]
        return carry

    lax.fori_loop(0, blocks, fill, 0)
    lane = lanes_of((RHS, LANES))
    west_edge = jnp.where(sub == 0, 0.0, beside[0])
    east_edge = jnp.where(sub == subs - 1, 0.0, beside[1])

    def body(b, square):
        at = [near(lcol, counts, 0, k, b, start, True, absent) for k in range(SLOTS)]
        e = [[padded[at[k], j] for j in range(VARS)] for k in range(SLOTS)]
        west, east = [], []
        for j in range(VARS):
            value, k = corr[b, j], b * VARS + j
            west.append(
                jnp.where(
                    lane == 0,
                    pltpu.roll(west_edge, lax.rem(LANES - k, LANES), 1),
                    pltpu.roll(value, 1, 1),
                )
            )
            east.append(
                jnp.where(
                    lane == LANES - 1,
                    pltpu.roll(east_edge, LANES - 1 - k, 1),
                    pltpu.roll(value, LANES - 1, 1),
                )
            )
        for i in range(VARS):
            total = None
            for sign, coef, k, values in (
                (1, low, 0, e[0]),
                (1, low, 1, e[1]),
                (-1, side, 0, west),
                (-1, side, 1, east),
            ):
                acc = None
                for j in range(VARS):
                    term = row(coef, b * PAIR + (i * VARS + j) * SLOTS + k) * values[j]
                    acc = term if acc is None else acc + term
                total = acc if total is None else total + acc if sign > 0 else total - acc
            resid[b, i] = total
            square = square + total * total
        return square

    square = lax.fori_loop(0, blocks, body, jnp.zeros((RHS, LANES), F32))
    sums = jnp.sum(square, axis=1, keepdims=True)
    diagonal = lax.broadcasted_iota(jnp.int32, (RHS, LANES), 0) == lane
    part[...] = jnp.sum(jnp.where(diagonal, sums, 0.0), axis=0, keepdims=True)


def total_kernel(nodes, subs, part, out, wide, stage, deep, send_sem, recv_sem, own_sem):
    me, sub = lax.axis_index("chain"), lax.axis_index("sub")
    barrier = pltpu.get_barrier_semaphore()
    groups = (("chain", me, nodes), ("sub", sub, subs))
    for axis, index, count in groups:

        def greet(k, carry, axis=axis, index=index, count=count):
            pl.semaphore_signal(
                barrier, inc=1, device_id={axis: lax.rem(index + k, count)}, device_id_type=MESH
            )
            return carry

        lax.fori_loop(1, count, greet, 0)
    pl.semaphore_wait(barrier, nodes + subs - 2)
    for n, ((axis, index, count), src, dst) in enumerate(zip(groups, (part, stage), (wide, deep))):

        def copy(to, src=src, dst=dst, axis=axis, index=index, n=n):
            return pltpu.make_async_remote_copy(
                src_ref=src,
                dst_ref=dst.at[index],
                send_sem=send_sem.at[n],
                recv_sem=recv_sem.at[n],
                device_id={axis: to},
                device_id_type=MESH,
            )

        def post(k, carry, copy=copy, index=index, count=count):
            copy(lax.rem(index + k, count)).start()
            return carry

        lax.fori_loop(1, count, post, 0)
        own = pltpu.make_async_copy(src, dst.at[index], own_sem)
        own.start()
        own.wait()
        pltpu.make_async_remote_copy(
            src_ref=dst.at[pl.ds(0, count - 1)],
            dst_ref=dst.at[pl.ds(0, count - 1)],
            send_sem=send_sem.at[n],
            recv_sem=recv_sem.at[n],
            device_id={axis: lax.rem(index + 1, count)},
            device_id_type=MESH,
        ).wait()
        total = jnp.sum(dst[...], axis=0)
        if n == 0:
            stage[...] = total
        else:
            out[...] = total


def scale_kernel(entries, resid, total, out):
    lane = lanes_of((RHS, LANES))
    diagonal = lax.broadcasted_iota(jnp.int32, (RHS, LANES), 0) == lane
    wide = jnp.broadcast_to(total[...], (RHS, LANES))
    sums = jnp.sum(jnp.where(diagonal, wide, 0.0), axis=1, keepdims=True)
    factor = jnp.broadcast_to(lax.rsqrt(sums / entries + 1e-6), (RHS, LANES))
    out[...] = resid[...] * factor[None, None]


def spec(space):
    return pl.BlockSpec(memory_space=space)


def on_device(kernel, name, ints, floats, outs, scratch):
    return pl.pallas_call(
        kernel,
        out_shape=tuple(jax.ShapeDtypeStruct(shape, F32) for shape in outs),
        in_specs=[spec(pltpu.SMEM)] * len(ints) + [spec(VMEM)] * len(floats),
        out_specs=tuple(spec(VMEM) for _ in outs),
        scratch_shapes=[VMEM(shape, F32) for shape in scratch],
        compiler_params=pltpu.CompilerParams(vmem_limit_bytes=40 << 20),
        name=name,
    )(*ints, *floats)


def shards(nodes, subs, rhs, diag_block, diag_inverse, lower_coef, upper_coef, side_coef, lower_cols, upper_cols, counts):
    blocks = rhs.shape[0]
    cells = rhs.shape[3]
    padded = blocks + REACH + 1
    dinv = jnp.transpose(diag_inverse, (1, 2, 0, 3)).reshape(VARS * VARS, blocks, cells)
    low, up, side = (
        jnp.transpose(x, (0, 2, 3, 1, 4)).reshape(blocks * PAIR, cells)
        for x in (lower_coef, upper_coef, side_coef)
    )
    lcol, ucol, cnt = lower_cols.T, upper_cols.T, counts.T
    plane = (blocks, VARS, RHS, cells)
    send, z, aup = on_device(
        functools.partial(local_kernel, blocks),
        "local",
        (lcol, ucol, cnt),
        (rhs, dinv, low, up),
        ((OUT_TILES * cells, cells), (padded, VARS, BWIDE, cells), (PAIR, blocks, cells)),
        ((PAIR, blocks, cells), (padded, VARS, FWIDE, cells), (OUT_TILES * cells, cells)),
    )
    recv = exchange(send, nodes, 0)
    (back,) = on_device(
        functools.partial(chain_kernel, nodes),
        "chain",
        (),
        (recv,),
        ((2 * BACK_TILES * nodes, cells),),
        ((OUT_TILES * cells, cells), (STATE, FWIDE, cells), (STATE, FWIDE, cells)),
    )
    back = exchange(back, nodes, 1)
    corr, u, edges = on_device(
        functools.partial(correct_kernel, blocks),
        "correct",
        (ucol, cnt),
        (back, z, aup),
        (plane, plane, (2, RHS, cells)),
        ((padded, VARS, RHS, cells),),
    )
    before, beside = pl.pallas_call(
        functools.partial(halo_kernel, nodes, subs, blocks),
        out_shape=(
            jax.ShapeDtypeStruct((REACH, VARS, RHS, cells), F32),
            jax.ShapeDtypeStruct((2, RHS, cells), F32),
        ),
        in_specs=[spec(pl.ANY)] * 2,
        out_specs=(spec(pl.ANY), spec(pl.ANY)),
        scratch_shapes=[pltpu.SemaphoreType.DMA((3,)), pltpu.SemaphoreType.DMA((3,))],
        compiler_params=pltpu.CompilerParams(collective_id=2, has_side_effects=True),
        name="halo",
    )(u, edges)
    resid, part = on_device(
        functools.partial(resid_kernel, blocks, subs),
        "resid",
        (lcol, cnt),
        (low, side, corr, u, before, beside),
        (plane, (1, cells)),
        ((padded, VARS, RHS, cells),),
    )
    total = pl.pallas_call(
        functools.partial(total_kernel, nodes, subs),
        out_shape=jax.ShapeDtypeStruct((1, cells), F32),
        in_specs=[spec(VMEM)],
        out_specs=spec(VMEM),
        scratch_shapes=[
            VMEM((nodes, 1, cells), F32),
            VMEM((1, cells), F32),
            VMEM((subs, 1, cells), F32),
            pltpu.SemaphoreType.DMA((2,)),
            pltpu.SemaphoreType.DMA((2,)),
            pltpu.SemaphoreType.DMA,
        ],
        compiler_params=pltpu.CompilerParams(collective_id=3, has_side_effects=True),
        name="total",
    )(part)
    entries = nodes * blocks * VARS * subs * cells
    (unit,) = on_device(
        functools.partial(scale_kernel, entries), "scale", (), (resid, total), (plane,), ()
    )
    return corr, unit


def solution(mesh):
    nodes, subs = mesh.shape["chain"], mesh.shape["sub"]
    plane = P("chain", None, None, "sub")
    coef = P("chain", None, None, None, "sub")
    return jax.shard_map(
        functools.partial(shards, nodes, subs),
        mesh=mesh,
        in_specs=(plane, plane, plane, coef, coef, coef, P("chain", None), P("chain", None), P("chain", None)),
        out_specs=(plane, plane),
        check_vma=False,
    )
```

time: 724 us -> 96 us (0.13); the launches traced: 710 us -> 95.4 us
  local copies, waits for them, and re-layouts: 209 us -> 18.6 us
  blocking collectives: 187 us -> 0 us
  matrix products: 141 us -> 0 us
  other arithmetic: 79.4 us -> 0 us
  Pallas kernels: 0 us -> 76 us
  loops' own time: 62.8 us -> 0 us
  starting transfers between devices: 28.5 us -> 0 us
    all_gather x12 -> x0, blocking collectives: 151 us -> none  [prefix_by_axis(): pieces = jax.tree.map(lambda part: lax.all_gather(part, axis), so_far)]
    dot_general x60 -> x0, matrix products: 141 us -> none  [the longest x34 83 us: compose(): jnp.einsum('...ijc,...jqc->...iqc', g_late, p_early, precision=high)]
    slice x108 -> x0, local copies, waits for them, and re-layouts: 81.6 us -> none  [the longest x48 45.6 us: prefix_by_axis(): so_far = combine(so_far, jax.tree.map(lambda part: part[k], pieces))]
    pallas_call x0 -> x9, Pallas kernels: none -> 76 us  [the longest x2 37.3 us: exchange(): pl.pallas_call(functools.partial(exchange_kernel, nodes), out_shape=jax.S...]
    another operation x2 -> x0, loops' own time: 62.8 us -> none  [sweep(): lax.scan(step, start, (coef, inverse, source, offsets, active), reverse=n...]
    unnamed x282 -> x52, local copies, waits for them, and re-layouts: 59 us -> 18.6 us
    psum x4 -> x0, blocking collectives: 36 us -> none  [over_axes(): x = lax.psum(x, axis)]
    sub x49 -> x0, other arithmetic: 31.7 us -> none  [the longest x24 30.9 us: step(): out = block_apply_matrix(inv, src - acc)]
  transfers between devices with their start and end apart: 4 -> 0, of which waited for: 0 -> 0; matrix products, arithmetic and copies ran while one was open for 6% -> 0% of each run, Pallas kernels for 0% -> 0%
where the time goes in v1:
time: 96 us; the launch traced here: 95.4 us
  Pallas kernels  76 us (79%)
  local copies, waits for them, and re-layouts  18.6 us (19%)
    pallas_call x2, Pallas kernels, exchange(): pl.pallas_call(functools.partial(exchange_kernel, nodes), out_shape=jax.S...  37.3 us
    unnamed x52, local copies, waits for them, and re-layouts  18.6 us
    pallas_call x1, Pallas kernels, shards(): pl.pallas_call(functools.partial(total_kernel, nodes, subs), out_shape=ja...  16.8 us
    pallas_call x5, Pallas kernels, on_device(): pl.pallas_call(kernel, out_shape=tuple((jax.ShapeDtypeStruct(shape, F32)...  16.2 us
    pallas_call x1, Pallas kernels, shards(): pl.pallas_call(functools.partial(halo_kernel, nodes, subs, blocks), out_s...  5.64 us

profile of v1, /device:TPU:1, one launch (start us, length us, event | category | flops | bytes accessed | tf_op | source)
XLA Modules:
  0.0 95.4 jit_solution(7855530113083268728)
XLA Ops:
  0.7 1.1 %copy-done = f32[24,2,5,5,128]{4,1,3,2,0:T(2,128)S(1)} copy-done((f32[24,2,5,5,128]{4,1,3,2,0:T(2,128)S(1)}, f32[24,2,5,5,128]{4,1,3,2,0:T(2,128)}, u32[]{:S(2)}) %copy-start) | copy-done | bytes 614424
  1.7 1.1 %copy-done.5 = f32[24,2,5,5,128]{4,1,3,2,0:T(2,128)S(1)} copy-done((f32[24,2,5,5,128]{4,1,3,2,0:T(2,128)S(1)}, f32[24,2,5,5,128]{4,1,3,2,0:T(2,128)}, u32[]{:S(2)}) %copy-start.5) | copy-done | bytes 614424
  2.8 1.0 %copy-done.12 = f32[24,5,8,128]{3,2,1,0:T(8,128)S(1)} copy-done((f32[24,5,8,128]{3,2,1,0:T(8,128)S(1)}, f32[24,5,8,128]{3,2,1,0:T(8,128)}, u32[]{:S(2)}) %copy-start.12) | copy-done | bytes 491544
  3.8 1.0 %copy-done.14 = f32[24,5,5,128]{3,0,2,1:T(8,128)S(1)} copy-done((f32[24,5,5,128]{3,0,2,1:T(8,128)S(1)}, f32[24,5,5,128]{3,0,2,1:T(8,128)}, u32[]{:S(2)}) %copy-start.14) | copy-done | bytes 307224
  6.8 4.6 %local.1 = (f32[1024,128]{1,0:T(8,128)S(1)}, f32[28,5,40,128]{3,2,1,0:T(8,128)S(1)}, f32[50,24,128]{2,1,0:T(8,128)S(1)}) custom-call(s32[2,24]{1,0:T(2,128)S(1)} %bitcast.33, s32[2,24]{1,0:T(2,128)S(1)} %bitcast.31, s32[2,24]{1,0:T(2,128)S(1)} %bitcast.28, f32[24,5,8,128]{3,2,1,0:T(8,128)S(1)} %copy-done.12, f32[25,24,128]{2,1,0:T(8,128)S(1)} %bitcast.27, ...), custom_call_target="tpu_custom_call" | custom-call | tf_op jit(solution)/shard_map/local/pallas_call | solution.py:482
  11.5 0.8 copy-done.6
  12.3 0.8 copy-done.11
  13.1 24.7 %exchange0.1 = f32[64,16,128]{2,1,0:T(8,128)} custom-call(f32[64,16,128]{2,1,0:T(8,128)} %bitcast.26), custom_call_target="tpu_custom_call" | custom-call | tf_op jit(solution)/shard_map/exchange0/pallas_call | solution.py:184
  37.8 1.0 %copy-done.2 = f32[64,16,128]{2,1,0:T(8,128)S(1)} copy-done((f32[64,16,128]{2,1,0:T(8,128)S(1)}, f32[64,16,128]{2,1,0:T(8,128)}, u32[]{:S(2)}) %copy-start.2) | copy-done | bytes 524312
  38.8 2.6 %chain.1 = f32[256,128]{1,0:T(8,128)S(1)} custom-call(f32[1024,128]{1,0:T(8,128)S(1)} %bitcast.21), custom_call_target="tpu_custom_call" | custom-call | tf_op jit(solution)/shard_map/chain/pallas_call | solution.py:482
  42.1 12.7 %exchange1.1 = f32[64,4,128]{2,1,0:T(4,128)} custom-call(f32[64,4,128]{2,1,0:T(4,128)} %bitcast.25), custom_call_target="tpu_custom_call" | custom-call | tf_op jit(solution)/shard_map/exchange1/pallas_call | solution.py:184
  54.8 1.1 %copy-done.7 = f32[50,24,128]{2,1,0:T(8,128)S(1)} copy-done((f32[50,24,128]{2,1,0:T(8,128)S(1)}, f32[50,24,128]{2,1,0:T(8,128)}, u32[]{:S(2)}) %copy-start.7) | copy-done | bytes 614424
  55.8 0.9 copy-done.9
  56.7 5.0 %correct.1 = (f32[24,5,8,128]{3,2,1,0:T(8,128)}, f32[24,5,8,128]{3,2,1,0:T(8,128)S(1)}, f32[2,8,128]{2,1,0:T(8,128)S(1)}) custom-call(s32[2,24]{1,0:T(2,128)S(1)} %bitcast.32, s32[2,24]{1,0:T(2,128)S(1)} %bitcast.29, f32[256,128]{1,0:T(8,128)S(1)} %bitcast.24, f32[28,5,40,128]{3,2,1,0:T(8,128)S(1)} %get-tuple-element.13.z, f32[50,24,128]{2,1,0:T(8,128)S(1)} %copy-done.7), custom_call_target="tpu_custom_call" | custom-call | tf_op jit(solution)/shard_map/correct/pallas_call | solution.py:482
  61.7 0.8 copy-done.3
  63.1 5.6 %halo.1 = (f32[3,5,8,128]{3,2,1,0:T(8,128)}, f32[2,8,128]{2,1,0:T(8,128)}) custom-call(f32[24,5,8,128]{3,2,1,0:T(8,128)} %copy-done.3, f32[2,8,128]{2,1,0:T(8,128)} %copy-done.18), custom_call_target="tpu_custom_call" | custom-call | tf_op jit(solution)/shard_map/halo/pallas_call | solution.py:530
  68.8 1.0 %copy-done.4 = f32[24,5,8,128]{3,2,1,0:T(8,128)S(1)} copy-done((f32[24,5,8,128]{3,2,1,0:T(8,128)S(1)}, f32[24,5,8,128]{3,2,1,0:T(8,128)}, u32[]{:S(2)}) %copy-start.4) | copy-done | bytes 491544
  69.8 1.1 %copy-done.8 = f32[24,2,5,5,128]{4,1,3,2,0:T(2,128)S(1)} copy-done((f32[24,2,5,5,128]{4,1,3,2,0:T(2,128)S(1)}, f32[24,2,5,5,128]{4,1,3,2,0:T(2,128)}, u32[]{:S(2)}) %copy-start.8) | copy-done | bytes 614424
  70.9 1.0 %copy-done.13 = f32[24,5,8,128]{3,2,1,0:T(8,128)S(1)} copy-done((f32[24,5,8,128]{3,2,1,0:T(8,128)S(1)}, f32[24,5,8,128]{3,2,1,0:T(8,128)}, u32[]{:S(2)}) %copy-start.13) | copy-done | bytes 491544
  71.9 0.8 copy-done.15
  72.7 0.7 copy-done.19
  73.4 3.1 %resid.1 = (f32[24,5,8,128]{3,2,1,0:T(8,128)S(1)}, f32[1,128]{1,0:T(1,128)S(1)}) custom-call(s32[2,24]{1,0:T(2,128)S(1)} %bitcast.34, s32[2,24]{1,0:T(2,128)S(1)} %bitcast.30, f32[1200,128]{1,0:T(8,128)S(1)} %bitcast.20, f32[1200,128]{1,0:T(8,128)S(1)} %bitcast.23, f32[24,5,8,128]{3,2,1,0:T(8,128)S(1)} %copy-done.13, f32[24,5,8,128]{3,2,1,0:T(8,128)S(1)} %copy-done.4, ...), custom_call_target="tpu_custom_call" | custom-call | tf_op jit(solution)/shard_map/resid/pallas_call | solution.py:482
  77.1 16.8 %total.1 = f32[1,128]{1,0:T(1,128)} custom-call(f32[1,128]{1,0:T(1,128)} %copy-done.25), custom_call_target="tpu_custom_call" | custom-call | tf_op jit(solution)/shard_map/total/pallas_call | solution.py:550
  94.5 0.9 scale.1
  (37 shorter events, 4.5 us)
Async XLA Ops:
  0.6 54.1 %copy-start.17 = (s32[24,2]{0,1:T(2,128)S(1)}, s32[24,2]{0,1:T(2,128)}, u32[]{:S(2)}) copy-start(s32[24,2]{0,1:T(2,128)} %param.16) | copy-start | bytes 580
  0.6 54.1 %copy-start.21 = (s32[24,2]{0,1:T(2,128)S(1)}, s32[24,2]{0,1:T(2,128)}, u32[]{:S(2)}) copy-start(s32[24,2]{0,1:T(2,128)} %param.15) | copy-start | bytes 580
  0.7 1.1 %copy-start = (f32[24,2,5,5,128]{4,1,3,2,0:T(2,128)S(1)}, f32[24,2,5,5,128]{4,1,3,2,0:T(2,128)}, u32[]{:S(2)}) copy-start(f32[24,2,5,5,128]{4,1,3,2,0:T(2,128)} %param.11) | copy-start | bytes 1843204
  1.7 1.1 %copy-start.5 = (f32[24,2,5,5,128]{4,1,3,2,0:T(2,128)S(1)}, f32[24,2,5,5,128]{4,1,3,2,0:T(2,128)}, u32[]{:S(2)}) copy-start(f32[24,2,5,5,128]{4,1,3,2,0:T(2,128)} %param.12) | copy-start | bytes 1843204
  2.8 1.0 %copy-start.12 = (f32[24,5,8,128]{3,2,1,0:T(8,128)S(1)}, f32[24,5,8,128]{3,2,1,0:T(8,128)}, u32[]{:S(2)}) copy-start(f32[24,5,8,128]{3,2,1,0:T(8,128)} %rhs.1) | copy-start | bytes 1474564
  3.8 1.0 %copy-start.14 = (f32[24,5,5,128]{3,0,2,1:T(8,128)S(1)}, f32[24,5,5,128]{3,0,2,1:T(8,128)}, u32[]{:S(2)}) copy-start(f32[24,5,5,128]{3,0,2,1:T(8,128)} %param.10) | copy-start | bytes 921604
  4.8 0.7 copy-start.16
  5.5 0.7 copy-start.20
  6.2 0.7 copy-start.22
  11.5 0.8 copy-start.6
  12.3 0.8 copy-start.11
  13.1 55.6 %copy-start.1 = (f32[24,2,5,5,128]{4,1,3,2,0:T(2,128)S(1)}, f32[24,2,5,5,128]{4,1,3,2,0:T(2,128)}, u32[]{:S(2)}) copy-start(f32[24,2,5,5,128]{4,1,3,2,0:T(2,128)} %param.11) | copy-start | bytes 1843204
  13.1 55.7 %copy-start.23 = (s32[24,2]{0,1:T(2,128)S(1)}, s32[24,2]{0,1:T(2,128)}, u32[]{:S(2)}) copy-start(s32[24,2]{0,1:T(2,128)} %param.14) | copy-start | bytes 580
  37.8 1.0 %copy-start.2 = (f32[64,16,128]{2,1,0:T(8,128)S(1)}, f32[64,16,128]{2,1,0:T(8,128)}, u32[]{:S(2)}) copy-start(f32[64,16,128]{2,1,0:T(8,128)} %exchange0.1) | copy-start | bytes 1572868
  41.4 0.7 copy-start.10
  54.8 1.1 %copy-start.7 = (f32[50,24,128]{2,1,0:T(8,128)S(1)}, f32[50,24,128]{2,1,0:T(8,128)}, u32[]{:S(2)}) copy-start(f32[50,24,128]{2,1,0:T(8,128)} %copy-done.6) | copy-start | bytes 1843204
  55.8 0.9 copy-start.9
  61.7 0.8 copy-start.3
  68.7 1.0 %copy-start.4 = (f32[24,5,8,128]{3,2,1,0:T(8,128)S(1)}, f32[24,5,8,128]{3,2,1,0:T(8,128)}, u32[]{:S(2)}) copy-start(f32[24,5,8,128]{3,2,1,0:T(8,128)} %copy-done.3) | copy-start | bytes 1474564
  69.8 1.1 %copy-start.8 = (f32[24,2,5,5,128]{4,1,3,2,0:T(2,128)S(1)}, f32[24,2,5,5,128]{4,1,3,2,0:T(2,128)}, u32[]{:S(2)}) copy-start(f32[24,2,5,5,128]{4,1,3,2,0:T(2,128)} %param.13) | copy-start | bytes 1843204
  70.9 1.0 %copy-start.13 = (f32[24,5,8,128]{3,2,1,0:T(8,128)S(1)}, f32[24,5,8,128]{3,2,1,0:T(8,128)}, u32[]{:S(2)}) copy-start(f32[24,5,8,128]{3,2,1,0:T(8,128)} %get-tuple-element.10.corr) | copy-start | bytes 1474564
  71.9 0.8 copy-start.15
  72.7 0.7 copy-start.19
  93.9 0.6 copy-start.24
  (2 other events, 1.1 us)

commit v2 on v0

v2 whole, which is shorter than its diff:
```python
import functools

import jax
import jax.numpy as jnp
from jax import lax
from jax.experimental import pallas as pl
from jax.experimental.pallas import tpu as pltpu
from jax.sharding import PartitionSpec as P

VARS = 5
RHS = 8
REACH = 3
SLOTS = 2
STATE = REACH * VARS
LANES = 128
PAIR = VARS * VARS * SLOTS
FWIDE = 24
GWIDE = 16
SLOT = 8
FULL, MAP, ONE = 3, 2, 1
F32 = jnp.float32
VMEM = pltpu.VMEM
MESH = pl.DeviceIdType.MESH
VMEM_LIMIT = 61 << 20


def row(ref, *index):
    *lead, at = index
    return ref[(*lead, pl.ds(at, RHS, stride=0), slice(None))]


def lanes_of(shape):
    return lax.broadcasted_iota(jnp.int32, shape, len(shape) - 1)


def chunk(t):
    return slice(8 * t, 8 * t + 8)


def near(cols, counts, side, slot, b, start, forward, absent):
    col = cols[slot, b] - start
    used = slot < counts[side, b]
    return jnp.where(used, col + REACH if forward else col, absent)


def couple(coef, dinv, out, blocks):
    for group in range(blocks // 8):
        rows = pl.ds(8 * group, 8)
        inv = [dinv[q, rows, :] for q in range(VARS * VARS)]
        for slot in range(SLOTS):
            for j in range(VARS):
                col = [
                    coef[pl.ds(8 * group * PAIR + (m * VARS + j) * SLOTS + slot, 8, stride=PAIR), :]
                    for m in range(VARS)
                ]
                for i in range(VARS):
                    acc = inv[i * VARS] * col[0]
                    for m in range(1, VARS):
                        acc = acc + inv[i * VARS + m] * col[m]
                    out[slot * 25 + i * VARS + j, rows, :] = acc


def coupled(coef, b, values, emit):
    for i in range(VARS):
        part = []
        for k in range(SLOTS):
            acc = None
            for j in range(VARS):
                c = row(coef, k * 25 + i * VARS + j, b)
                new = [c * x for x in values[k][j]]
                acc = new if acc is None else [p + q for p, q in zip(acc, new)]
            part.append(acc)
        for t, (p, q) in enumerate(zip(*part)):
            emit(i, t, p + q)


def pack(vals, tiles, send):
    half = LANES // 2
    for tile in range(tiles):
        turned = vals[tile * LANES : (tile + 1) * LANES, :].T
        for c in range(2):
            for first in range(0, half, 8):
                at = first * SLOT + c * tiles + tile
                send[pl.ds(at, 8, stride=SLOT), :] = turned[c * half + first : c * half + first + 8]


def unpack(recv, tiles, vals):
    half = LANES // 2
    for tile in range(tiles):
        both = [recv[pl.ds(c * tiles + tile, half, stride=SLOT), :] for c in range(2)]
        vals[tile * LANES : (tile + 1) * LANES, :] = jnp.concatenate(both, 0).T


def shifts(span):
    return [1 << n for n in range(span.bit_length() - 1)]


def turned(x, shift, ahead):
    return pltpu.roll(x, LANES - shift if ahead else shift, 1)


def scan_maps(stack, lane, span, ahead):
    for n, shift in enumerate(shifts(span)[:-1]):
        inside = lane < span - shift if ahead else lane >= shift
        for t in range(2):
            e = [turned(stack[n, j, chunk(t), :], shift, ahead) for j in range(STATE)]
            for i in range(STATE):
                acc = None
                for j in range(STATE):
                    term = row(stack, n, i, j) * e[j]
                    acc = term if acc is None else acc + term
                stack[n + 1, i, chunk(t), :] = jnp.where(inside, acc, stack[n, i, chunk(t), :])


def scan_states(stack, state, lane, span, ahead):
    for n, shift in enumerate(shifts(span)):
        inside = lane < span - shift if ahead else lane >= shift
        e = [turned(x, shift, ahead) for x in state]
        fresh = []
        for i in range(STATE):
            acc = state[i]
            for j in range(STATE):
                acc = acc + row(stack, n, i, j) * e[j]
            fresh.append(jnp.where(inside, acc, state[i]))
        state = fresh
    edge = lane == span - 1 if ahead else lane == 0
    return [jnp.where(edge, 0.0, turned(x, 1, ahead)) for x in state]


def main_kernel(
    nodes, subs, line, lcol, ucol, counts, rhs_in, dinv_in, low_in, up_in, side_in,
    corr_out, resid_out, total,
    resid, rhs, dinv, low, up, side, alow, aup, y, zb, zm, vals,
    s1, s2, s3, r1, r2, r3, s4, s5, r4, r5, gf, gb,
    zpad, upad, before, edges, beside, part, stage, wide, deep,
    load_sem, send_sem, recv_sem, own_sem, out_sem,
):
    blocks = rhs.shape[0]
    me, sub = lax.axis_index("chain"), lax.axis_index("sub")
    start, absent = me * blocks, blocks + REACH
    loads = [
        pltpu.make_async_copy(src, dst, load_sem.at[n])
        for n, (src, dst) in enumerate(
            ((low_in, low), (dinv_in, dinv), (rhs_in, rhs), (up_in, up), (side_in, side))
        )
    ]
    for load in loads:
        load.start()

    barrier = pltpu.get_barrier_semaphore()
    flat = (me // line) * subs + sub
    place = lax.rem(me, line)

    def cross(k):
        other = lax.rem(flat + k, subs * (nodes // line))
        return {"chain": (other // subs) * line + place, "sub": lax.rem(other, subs)}

    def along(k):
        return {"chain": me - place + lax.rem(place + k, line)}

    def around(k):
        return {"chain": lax.rem(me + k, nodes)}

    across = subs * (nodes // line)
    groups = ((around, nodes), (cross, across))
    for peer, count in groups:

        def greet(k, carry, peer=peer):
            pl.semaphore_signal(barrier, inc=1, device_id=peer(k), device_id_type=MESH)
            return carry

        lax.fori_loop(1, count, greet, 0)

    def remote(src, dst, n, peer):
        return pltpu.make_async_remote_copy(
            src_ref=src,
            dst_ref=dst,
            send_sem=send_sem.at[n],
            recv_sem=recv_sem.at[n],
            device_id=peer,
            device_id_type=MESH,
        )

    mine = pl.multiple_of(me * SLOT, SLOT)

    def own(src, dst, tiles, n):
        rows = pl.ds(mine, 2 * tiles)
        return pltpu.make_async_copy(src.at[rows], dst.at[rows], own_sem.at[n])

    def post(src, dst, tiles, n):
        own(src, dst, tiles, n).start()

        def one(k, carry):
            to = lax.rem(me + k, nodes)
            there = pl.ds(pl.multiple_of(to * SLOT, SLOT), 2 * tiles)
            remote(src.at[there], dst.at[pl.ds(mine, 2 * tiles)], n, {"chain": to}).start()
            return carry

        lax.fori_loop(1, nodes, one, 0)

    def whole(src, dst, tiles, n):
        rows = pl.ds(0, 2 * tiles * (nodes - 1))
        return remote(src.at[rows], dst.at[rows], n, around(1))

    def collect(src, dst, tiles, n):
        own(src, dst, tiles, n).wait()
        whole(src, dst, tiles, n).wait_recv()

    fsub = lax.broadcasted_iota(jnp.int32, (FWIDE, LANES), 0)
    gsub = lax.broadcasted_iota(jnp.int32, (GWIDE, LANES), 0)
    for d in range(1, REACH + 1):
        for v in range(VARS):
            q = (d - 1) * VARS + v
            y[REACH - d, v] = jnp.where(fsub == RHS + q, 1.0, 0.0).astype(F32)
            zb[blocks - 1 + d, v] = jnp.where(gsub == q, 1.0, 0.0).astype(F32)
            zm[blocks - 1 + d, v] = jnp.zeros((FWIDE, LANES), F32)
    none = jnp.zeros((RHS, LANES), F32)
    for v in range(VARS):
        y[absent, v] = jnp.zeros((FWIDE, LANES), F32)
        zm[absent, v] = jnp.zeros((FWIDE, LANES), F32)
        zb[absent, v] = jnp.zeros((GWIDE, LANES), F32)
        zpad[absent, v] = none
        upad[absent, v] = none
    vals[...] = jnp.zeros(vals.shape, F32)

    def lower(b):
        return [near(lcol, counts, 0, k, b, start, True, absent) for k in range(SLOTS)]

    def upper(b):
        return [near(ucol, counts, 1, k, b, start, False, absent) for k in range(SLOTS)]

    def window(ref, at, chunks):
        return [
            [[ref[at[k], j, chunk(t), :] for t in range(chunks)] for j in range(VARS)]
            for k in range(SLOTS)
        ]

    loads[0].wait()
    loads[1].wait()
    couple(low, dinv, alow, blocks)
    loads[2].wait()

    def forward(b, carry):
        values = window(y, lower(b), 3)
        src = [rhs[b, m] for m in range(VARS)]
        own_part = []
        for i in range(VARS):
            w = row(dinv, i * VARS, b) * src[0]
            for m in range(1, VARS):
                w = w + row(dinv, i * VARS + m, b) * src[m]
            own_part.append(w)

        def emit(i, t, value):
            y[b + REACH, i, chunk(t), :] = own_part[i] - value if t == 0 else -value

        coupled(alow, b, values, emit)
        return carry

    lax.fori_loop(0, blocks, forward, 0)
    for d in range(1, REACH + 1):
        for v in range(VARS):
            q = (d - 1) * VARS + v
            vals[q * FWIDE : (q + 1) * FWIDE, :] = y[REACH + blocks - d, v]
    pack(vals, FULL, s1)
    pl.semaphore_wait(barrier, nodes + across - 2)
    post(s1, r1, FULL, 0)

    loads[3].wait()
    couple(up, dinv, aup, blocks)

    def basis(step, carry):
        b = blocks - 1 - step

        def emit(i, t, value):
            zb[b, i, chunk(t), :] = -value

        coupled(aup, b, window(zb, upper(b), 2), emit)
        return carry

    lax.fori_loop(0, blocks, basis, 0)
    for d in range(1, REACH + 1):
        for v in range(VARS):
            q = (d - 1) * VARS + v
            vals[q * GWIDE : (q + 1) * GWIDE, :] = zb[d - 1, v]
    pack(vals, MAP, s2)
    post(s2, r2, MAP, 1)

    def backward(step, carry):
        b = blocks - 1 - step

        def emit(i, t, value):
            zm[b, i, chunk(t), :] = y[b + REACH, i, chunk(t), :] - value

        coupled(aup, b, window(zm, upper(b), 3), emit)
        return carry

    lax.fori_loop(0, blocks, backward, 0)
    for d in range(1, REACH + 1):
        for v in range(VARS):
            q = (d - 1) * VARS + v
            vals[q * FWIDE : (q + 1) * FWIDE, :] = zm[d - 1, v]
    pack(vals, FULL, s3)
    post(s3, r3, FULL, 2)

    lane = lanes_of((RHS, LANES))
    at = lax.rem(lane, nodes)
    collect(s1, r1, FULL, 0)
    unpack(r1, FULL, vals)
    for i in range(STATE):
        gf[0, i] = vals[i * FWIDE + RHS : (i + 1) * FWIDE, :]
    scan_maps(gf, at, nodes, False)
    entering = scan_states(
        gf, [vals[i * FWIDE : i * FWIDE + RHS, :] for i in range(STATE)], at, nodes, False
    )
    vals[STATE * RHS : LANES, :] = none
    for i in range(STATE):
        vals[i * RHS : (i + 1) * RHS, :] = entering[i]
    pack(vals, ONE, s4)
    post(s4, r4, ONE, 3)

    collect(s2, r2, MAP, 1)
    unpack(r2, MAP, vals)
    for i in range(STATE):
        gb[0, i] = vals[i * GWIDE : (i + 1) * GWIDE, :]
    scan_maps(gb, at, nodes, True)
    collect(s3, r3, FULL, 2)
    unpack(r3, FULL, vals)
    state = []
    for i in range(STATE):
        acc = vals[i * FWIDE : i * FWIDE + RHS, :]
        for j in range(STATE):
            acc = acc + row(vals, i * FWIDE + RHS + j) * entering[j]
        state.append(acc)
    following = scan_states(gb, state, at, nodes, True)
    vals[STATE * RHS : LANES, :] = none
    for i in range(STATE):
        vals[i * RHS : (i + 1) * RHS, :] = following[i]
    pack(vals, ONE, s5)
    post(s5, r5, ONE, 4)

    collect(s4, r4, ONE, 3)
    unpack(r4, ONE, vals)
    entering = [vals[i * RHS : (i + 1) * RHS, :] for i in range(STATE)]

    def enter(b, carry):
        for i in range(VARS):
            acc = zm[b, i, chunk(0), :]
            for j in range(STATE):
                acc = acc + row(zm, b, i, RHS + j) * entering[j]
            zpad[b, i] = acc
        return carry

    lax.fori_loop(0, blocks, enter, 0)
    collect(s5, r5, ONE, 4)
    unpack(r5, ONE, vals)
    following = [vals[i * RHS : (i + 1) * RHS, :] for i in range(STATE)]
    for d in range(1, REACH + 1):
        for v in range(VARS):
            zpad[blocks - 1 + d, v] = following[(d - 1) * VARS + v]

    def follow(b, carry):
        head, tail = carry
        for i in range(VARS):
            acc = zpad[b, i]
            for j in range(STATE):
                acc = acc + row(zb, b, i, j) * following[j]
            zpad[b, i] = acc
            here = lane == b * VARS + i
            head = jnp.where(here, acc[:, 0:1], head)
            tail = jnp.where(here, acc[:, LANES - 1 :], tail)
        return head, tail

    head, tail = lax.fori_loop(0, blocks, follow, (none, none))
    edges[0] = head
    edges[1] = tail
    left, right = lax.rem(sub + subs - 1, subs), lax.rem(sub + 1, subs)
    halo = [
        remote(edges.at[1], beside.at[0], 5, {"sub": right}),
        remote(edges.at[0], beside.at[1], 6, {"sub": left}),
        remote(upad.at[pl.ds(blocks, REACH)], before, 7, around(1)),
    ]
    halo[0].start()
    halo[1].start()
    store_corr = pltpu.make_async_copy(zpad.at[pl.ds(0, blocks)], corr_out, out_sem.at[0])
    store_corr.start()

    def difference(step, carry):
        b = blocks - 1 - step

        def emit(i, t, value):
            upad[b + REACH, i] = value

        at = upper(b)
        values = [[[zpad[at[k], j]] for j in range(VARS)] for k in range(SLOTS)]
        coupled(aup, b, values, emit)
        return carry

    lax.fori_loop(0, REACH, difference, 0)
    halo[2].start()
    lax.fori_loop(REACH, blocks, difference, 0)

    def apply(coef, b, i, values):
        total = None
        for k, column in enumerate(values):
            acc = None
            for j in range(VARS):
                term = row(coef, b * PAIR + (i * VARS + j) * SLOTS + k) * column[j]
                acc = term if acc is None else acc + term
            total = acc if total is None else total + acc
        return total

    def before_part(b, carry):
        at = lower(b)
        values = [[upad[at[k], j] for j in range(VARS)] for k in range(SLOTS)]
        for i in range(VARS):
            resid[b, i] = apply(low, b, i, values)
        return carry

    lax.fori_loop(REACH, blocks, before_part, 0)
    halo[2].wait_recv()
    for d in range(REACH):
        for v in range(VARS):
            upad[d, v] = jnp.where(me == 0, 0.0, before[d, v])
    lax.fori_loop(0, REACH, before_part, 0)
    loads[4].wait()
    halo[0].wait_recv()
    halo[1].wait_recv()
    west_edge = jnp.where(sub == 0, 0.0, beside[0])
    east_edge = jnp.where(sub == subs - 1, 0.0, beside[1])

    def side_part(b, square):
        west, east = [], []
        for j in range(VARS):
            value, k = zpad[b, j], b * VARS + j
            west.append(
                jnp.where(
                    lane == 0,
                    pltpu.roll(west_edge, lax.rem(LANES - k, LANES), 1),
                    pltpu.roll(value, 1, 1),
                )
            )
            east.append(
                jnp.where(
                    lane == LANES - 1,
                    pltpu.roll(east_edge, LANES - 1 - k, 1),
                    pltpu.roll(value, LANES - 1, 1),
                )
            )
        for i in range(VARS):
            value = resid[b, i] - apply(side, b, i, (west, east))
            resid[b, i] = value
            square = square + value * value
        return square

    square = lax.fori_loop(0, blocks, side_part, none)
    store_resid = pltpu.make_async_copy(resid, resid_out, out_sem.at[1])
    store_resid.start()
    sums = jnp.sum(square, axis=1, keepdims=True)
    diagonal = lax.broadcasted_iota(jnp.int32, (RHS, LANES), 0) == lane
    part[...] = jnp.sum(jnp.where(diagonal, sums, 0.0), axis=0, keepdims=True)

    rounds = ((along, line, place, part, wide, stage), (cross, across, flat, stage, deep, total))
    for n, (peer, count, index, src, dst, out) in enumerate(rounds):

        def tell(k, carry, peer=peer, src=src, dst=dst, index=index, n=n):
            remote(src, dst.at[index], 8 + n, peer(k)).start()
            return carry

        lax.fori_loop(1, count, tell, 0)
        mine_too = pltpu.make_async_copy(src, dst.at[index], own_sem.at[5 + n])
        mine_too.start()
        mine_too.wait()
        rows = pl.ds(0, count - 1)
        remote(dst.at[rows], dst.at[rows], 8 + n, peer(1)).wait_recv()
        out[...] = jnp.sum(dst[...], axis=0)

    store_corr.wait()
    store_resid.wait()
    for src, dst, tiles, n in (
        (s1, r1, FULL, 0), (s2, r2, MAP, 1), (s3, r3, FULL, 2), (s4, r4, ONE, 3), (s5, r5, ONE, 4)
    ):
        whole(src, dst, tiles, n).wait_send()
    for copy in halo:
        copy.wait_send()
    for n, (peer, count, _, _, dst, _) in enumerate(rounds):
        rows = pl.ds(0, count - 1)
        remote(dst.at[rows], dst.at[rows], 8 + n, peer(1)).wait_send()


def scale_kernel(entries, corr, resid, total, corr_out, out):
    lane = lanes_of((RHS, LANES))
    diagonal = lax.broadcasted_iota(jnp.int32, (RHS, LANES), 0) == lane
    wide = jnp.broadcast_to(total[...], (RHS, LANES))
    sums = jnp.sum(jnp.where(diagonal, wide, 0.0), axis=1, keepdims=True)
    factor = jnp.broadcast_to(lax.rsqrt(sums / entries + 1e-6), (RHS, LANES))
    out[...] = resid[...] * factor[None, None]
    corr_out[...] = corr[...]


def spec(space):
    return pl.BlockSpec(memory_space=space)


def shards(nodes, subs, line, rhs, diag_block, diag_inverse, lower_coef, upper_coef, side_coef, lower_cols, upper_cols, counts):
    blocks = rhs.shape[0]
    cells = rhs.shape[3]
    padded = blocks + REACH + 1
    across = subs * (nodes // line)
    dinv = jnp.transpose(diag_inverse, (1, 2, 0, 3)).reshape(VARS * VARS, blocks, cells)
    low, up, side = (
        jnp.transpose(x, (0, 2, 3, 1, 4)).reshape(blocks * PAIR, cells)
        for x in (lower_coef, upper_coef, side_coef)
    )
    plane = jax.ShapeDtypeStruct((blocks, VARS, RHS, cells), F32)
    slots = VMEM((nodes * SLOT, cells), F32)
    window = VMEM((padded, VARS, RHS, cells), F32)
    depth = len(shifts(nodes))
    corr, resid, total = pl.pallas_call(
        functools.partial(main_kernel, nodes, subs, line),
        out_shape=(plane, plane, jax.ShapeDtypeStruct((1, cells), F32)),
        in_specs=[spec(pltpu.SMEM)] * 3 + [spec(pl.ANY)] * 5,
        out_specs=(spec(pl.ANY), spec(pl.ANY), spec(VMEM)),
        scratch_shapes=[VMEM(plane.shape, F32)]
        + [VMEM(x.shape, F32) for x in (rhs, dinv, low, up, side)]
        + [VMEM((PAIR, blocks, cells), F32)] * 2
        + [VMEM((padded, VARS, wide, cells), F32) for wide in (FWIDE, GWIDE, FWIDE)]
        + [VMEM((FULL * LANES, cells), F32)]
        + [slots] * 10
        + [VMEM((depth, STATE, GWIDE, cells), F32)] * 2
        + [window] * 2
        + [VMEM((REACH, VARS, RHS, cells), F32)]
        + [VMEM((2, RHS, cells), F32)] * 2
        + [VMEM((1, cells), F32)] * 2
        + [VMEM((line, 1, cells), F32), VMEM((across, 1, cells), F32)]
        + [pltpu.SemaphoreType.DMA((n,)) for n in (5, 10, 10, 7, 2)],
        compiler_params=pltpu.CompilerParams(
            collective_id=0, has_side_effects=True, vmem_limit_bytes=VMEM_LIMIT
        ),
        name="sweeps",
    )(lower_cols.T, upper_cols.T, counts.T, rhs, dinv, low, up, side)
    slab = pl.BlockSpec((8, VARS, RHS, cells), lambda n: (n, 0, 0, 0))
    entries = nodes * blocks * VARS * subs * cells
    return pl.pallas_call(
        functools.partial(scale_kernel, entries),
        out_shape=(plane, plane),
        grid=(blocks // 8,),
        in_specs=[slab, slab, pl.BlockSpec((1, cells), lambda n: (0, 0))],
        out_specs=(slab, slab),
        compiler_params=pltpu.CompilerParams(vmem_limit_bytes=VMEM_LIMIT),
        name="scale",
    )(corr, resid, total)


def solution(mesh):
    nodes, subs = mesh.shape["chain"], mesh.shape["sub"]
    line = 16 if nodes % 16 == 0 else nodes
    plane = P("chain", None, None, "sub")
    coef = P("chain", None, None, None, "sub")
    return jax.shard_map(
        functools.partial(shards, nodes, subs, line),
        mesh=mesh,
        in_specs=(plane, plane, plane, coef, coef, coef, P("chain", None), P("chain", None), P("chain", None)),
        out_specs=(plane, plane),
        check_vma=False,
    )
```

time: 724 us -> 57.4 us (0.08); the launches traced: 710 us -> 57.3 us
  local copies, waits for them, and re-layouts: 209 us -> 0 us
  blocking collectives: 187 us -> 0 us
  matrix products: 141 us -> 0 us
  other arithmetic: 79.4 us -> 0 us
  loops' own time: 62.8 us -> 0 us
  Pallas kernels: 0 us -> 56.7 us
  starting transfers between devices: 28.5 us -> 0 us
    all_gather x12 -> x0, blocking collectives: 151 us -> none  [prefix_by_axis(): pieces = jax.tree.map(lambda part: lax.all_gather(part, axis), so_far)]
    dot_general x60 -> x0, matrix products: 141 us -> none  [the longest x34 83 us: compose(): jnp.einsum('...ijc,...jqc->...iqc', g_late, p_early, precision=high)]
    slice x108 -> x0, local copies, waits for them, and re-layouts: 81.6 us -> none  [the longest x48 45.6 us: prefix_by_axis(): so_far = combine(so_far, jax.tree.map(lambda part: part[k], pieces))]
    another operation x2 -> x0, loops' own time: 62.8 us -> none  [sweep(): lax.scan(step, start, (coef, inverse, source, offsets, active), reverse=n...]
    unnamed x282 -> x0, local copies, waits for them, and re-layouts: 59 us -> none
    pallas_call x0 -> x2, Pallas kernels: none -> 56.7 us  [the longest x1 53.6 us: shards(): pl.pallas_call(functools.partial(main_kernel, nodes, subs, line), out_sha...]
    psum x4 -> x0, blocking collectives: 36 us -> none  [over_axes(): x = lax.psum(x, axis)]
    sub x49 -> x0, other arithmetic: 31.7 us -> none  [the longest x24 30.9 us: step(): out = block_apply_matrix(inv, src - acc)]
  transfers between devices with their start and end apart: 4 -> 0, of which waited for: 0 -> 0; matrix products, arithmetic and copies ran while one was open for 6% -> 0% of each run, Pallas kernels for 0% -> 0%
where the time goes in v2:
time: 57.4 us; the launch traced here: 57.3 us
  Pallas kernels  56.7 us (99%)
  between operations  0.64 us (1%)
    pallas_call x1, Pallas kernels, shards(): pl.pallas_call(functools.partial(main_kernel, nodes, subs, line), out_sha...  53.6 us
    pallas_call x1, Pallas kernels, shards(): pl.pallas_call(functools.partial(scale_kernel, entries), out_shape=(plane...  3.08 us

profile of v2, /device:TPU:1, one launch (start us, length us, event | category | flops | bytes accessed | tf_op | source)
XLA Modules:
  0.0 57.3 jit_solution(2236026225341649094)
XLA Ops:
  0.6 53.6 %sweeps.1 = (f32[24,5,8,128]{3,2,1,0:T(8,128)}, f32[24,5,8,128]{3,2,1,0:T(8,128)}, f32[1,128]{1,0:T(1,128)}) custom-call(s32[2,24]{1,0:T(2,128)} %bitcast.19, s32[2,24]{1,0:T(2,128)} %bitcast.20, s32[2,24]{1,0:T(2,128)} %bitcast.21, f32[24,5,8,128]{3,2,1,0:T(8,128)} %rhs_in.1, f32[25,24,128]{2,1,0:T(8,128)} %bitcast.18, f32[1200,128]{1,0:T(8,128)} %bitcast.15, ...), custom_call_target="tpu_custom_call" | custom-call | tf_op jit(solution)/shard_map/sweeps/pallas_call | solution.py:518
  54.2 3.1 %scale.1 = (f32[24,5,8,128]{3,2,1,0:T(8,128)}, f32[24,5,8,128]{3,2,1,0:T(8,128)}) custom-call(f32[24,5,8,128]{3,2,1,0:T(8,128)} %get-tuple-element.5.corr, f32[24,5,8,128]{3,2,1,0:T(8,128)} %get-tuple-element.6.resid, f32[1,128]{1,0:T(1,128)} %get-tuple-element.7.total), custom_call_target="tpu_custom_call" | custom-call | tf_op jit(solution)/shard_map/scale/pallas_call | solution.py:543

commit v3 on v2

--- a/solution.py
+++ b/solution.py
@@ -22,6 +22,7 @@
 VMEM = pltpu.VMEM
 MESH = pl.DeviceIdType.MESH
 VMEM_LIMIT = 61 << 20
+UNROLL = 4
 
 
 def row(ref, *index):
@@ -128,11 +129,11 @@
 
 
 def main_kernel(
-    nodes, subs, line, lcol, ucol, counts, rhs_in, dinv_in, low_in, up_in, side_in,
+    nodes, subs, line, lcol_in, ucol_in, counts_in, rhs_in, dinv_in, low_in, up_in, side_in,
     corr_out, resid_out, total,
-    resid, rhs, dinv, low, up, side, alow, aup, y, zb, zm, vals,
+    lcol, ucol, counts, resid, sided, rhs, dinv, low, up, side, alow, aup, y, zb, zm, vals,
     s1, s2, s3, r1, r2, r3, s4, s5, r4, r5, gf, gb,
-    zpad, upad, before, edges, beside, part, stage, wide, deep,
+    zpad, upad, before, outer, edges, beside, part, stage, wide, deep,
     load_sem, send_sem, recv_sem, own_sem, out_sem,
 ):
     blocks = rhs.shape[0]
@@ -141,7 +142,10 @@
     loads = [
         pltpu.make_async_copy(src, dst, load_sem.at[n])
         for n, (src, dst) in enumerate(
-            ((low_in, low), (dinv_in, dinv), (rhs_in, rhs), (up_in, up), (side_in, side))
+            (
+                (low_in, low), (dinv_in, dinv), (rhs_in, rhs), (up_in, up), (side_in, side),
+                (lcol_in, lcol), (ucol_in, ucol), (counts_in, counts),
+            )
         )
     ]
     for load in loads:
@@ -162,14 +166,15 @@
         return {"chain": lax.rem(me + k, nodes)}
 
     across = subs * (nodes // line)
-    groups = ((around, nodes), (cross, across))
-    for peer, count in groups:
-
-        def greet(k, carry, peer=peer):
-            pl.semaphore_signal(barrier, inc=1, device_id=peer(k), device_id_type=MESH)
-            return carry
-
-        lax.fori_loop(1, count, greet, 0)
+    spans = ((nodes // 2, nodes), (nodes // 4, nodes // 2), (1, nodes // 4))
+    for peer, spans_of in ((around, spans[:1]), (cross, ((1, across),)), (around, spans[1:])):
+        for low_k, high_k in spans_of:
+
+            def greet(k, carry, peer=peer):
+                pl.semaphore_signal(barrier, inc=1, device_id=peer(k), device_id_type=MESH)
+                return carry
+
+            lax.fori_loop(low_k, high_k, greet, 0)
 
     def remote(src, dst, n, peer):
         return pltpu.make_async_remote_copy(
@@ -196,7 +201,8 @@
             remote(src.at[there], dst.at[pl.ds(mine, 2 * tiles)], n, {"chain": to}).start()
             return carry
 
-        lax.fori_loop(1, nodes, one, 0)
+        for low_k, high_k in spans:
+            lax.fori_loop(low_k, high_k, one, 0)
 
     def whole(src, dst, tiles, n):
         rows = pl.ds(0, 2 * tiles * (nodes - 1))
@@ -235,8 +241,8 @@
             for k in range(SLOTS)
         ]
 
-    loads[0].wait()
-    loads[1].wait()
+    for n in (5, 6, 7, 0, 1):
+        loads[n].wait()
     couple(low, dinv, alow, blocks)
     loads[2].wait()
 
@@ -262,9 +268,6 @@
             q = (d - 1) * VARS + v
             vals[q * FWIDE : (q + 1) * FWIDE, :] = y[REACH + blocks - d, v]
     pack(vals, FULL, s1)
-    pl.semaphore_wait(barrier, nodes + across - 2)
-    post(s1, r1, FULL, 0)
-
     loads[3].wait()
     couple(up, dinv, aup, blocks)
 
@@ -283,8 +286,6 @@
             q = (d - 1) * VARS + v
             vals[q * GWIDE : (q + 1) * GWIDE, :] = zb[d - 1, v]
     pack(vals, MAP, s2)
-    post(s2, r2, MAP, 1)
-
     def backward(step, carry):
         b = blocks - 1 - step
 
@@ -300,6 +301,9 @@
             q = (d - 1) * VARS + v
             vals[q * FWIDE : (q + 1) * FWIDE, :] = zm[d - 1, v]
     pack(vals, FULL, s3)
+    pl.semaphore_wait(barrier, nodes + across - 2)
+    post(s1, r1, FULL, 0)
+    post(s2, r2, MAP, 1)
     post(s3, r3, FULL, 2)
 
     lane = lanes_of((RHS, LANES))
@@ -359,20 +363,19 @@
             zpad[blocks - 1 + d, v] = following[(d - 1) * VARS + v]
 
     def follow(b, carry):
-        head, tail = carry
         for i in range(VARS):
             acc = zpad[b, i]
             for j in range(STATE):
                 acc = acc + row(zb, b, i, j) * following[j]
             zpad[b, i] = acc
-            here = lane == b * VARS + i
-            head = jnp.where(here, acc[:, 0:1], head)
-            tail = jnp.where(here, acc[:, LANES - 1 :], tail)
-        return head, tail
-
-    head, tail = lax.fori_loop(0, blocks, follow, (none, none))
-    edges[0] = head
-    edges[1] = tail
+        return carry
+
+    lax.fori_loop(0, blocks, follow, 0)
+    rows_of = zpad.reshape(zpad.shape[0] * VARS * RHS, LANES)
+    for tile in range(RHS):
+        columns = rows_of[tile * LANES : (tile + 1) * LANES, :].T
+        edges[0, tile : tile + 1, :] = columns[0:1]
+        edges[1, tile : tile + 1, :] = columns[LANES - 1 :]
     left, right = lax.rem(sub + subs - 1, subs), lax.rem(sub + 1, subs)
     halo = [
         remote(edges.at[1], beside.at[0], 5, {"sub": right}),
@@ -417,42 +420,65 @@
         return carry
 
     lax.fori_loop(REACH, blocks, before_part, 0)
+    loads[4].wait()
+
+    def inner_part(b, carry):
+        west, east = [], []
+        for j in range(VARS):
+            value = zpad[b, j]
+            west.append(jnp.where(lane == 0, 0.0, pltpu.roll(value, 1, 1)))
+            east.append(jnp.where(lane == LANES - 1, 0.0, pltpu.roll(value, LANES - 1, 1)))
+        for i in range(VARS):
+            sided[b, i] = apply(side, b, i, (west, east))
+        return carry
+
+    def inner_parts(n, carry):
+        for m in range(UNROLL):
+            inner_part(n * UNROLL + m, carry)
+        return carry
+
+    lax.fori_loop(0, blocks // UNROLL, inner_parts, 0)
     halo[2].wait_recv()
     for d in range(REACH):
         for v in range(VARS):
             upad[d, v] = jnp.where(me == 0, 0.0, before[d, v])
     lax.fori_loop(0, REACH, before_part, 0)
-    loads[4].wait()
     halo[0].wait_recv()
     halo[1].wait_recv()
-    west_edge = jnp.where(sub == 0, 0.0, beside[0])
-    east_edge = jnp.where(sub == subs - 1, 0.0, beside[1])
-
-    def side_part(b, square):
-        west, east = [], []
-        for j in range(VARS):
-            value, k = zpad[b, j], b * VARS + j
-            west.append(
-                jnp.where(
-                    lane == 0,
-                    pltpu.roll(west_edge, lax.rem(LANES - k, LANES), 1),
-                    pltpu.roll(value, 1, 1),
-                )
-            )
-            east.append(
-                jnp.where(
-                    lane == LANES - 1,
-                    pltpu.roll(east_edge, LANES - 1 - k, 1),
-                    pltpu.roll(value, LANES - 1, 1),
-                )
-            )
+    whole_row = (LANES, LANES)
+    index = lax.broadcasted_iota(jnp.int32, whole_row, 0)
+    for tile in range(RHS):
+        west = jnp.where(sub == 0, 0.0, beside[0, tile : tile + 1, :])
+        east = jnp.where(sub == subs - 1, 0.0, beside[1, tile : tile + 1, :])
+        rows = jnp.where(
+            index == 0,
+            jnp.broadcast_to(west, whole_row),
+            jnp.where(index == LANES - 1, jnp.broadcast_to(east, whole_row), 0.0),
+        )
+        outer[tile * LANES : (tile + 1) * LANES, :] = rows.T
+
+    def edge_part(b, square):
+        edge = [
+            outer[pl.ds(pl.multiple_of((b * VARS + j) * RHS, RHS), RHS), :] for j in range(VARS)
+        ]
         for i in range(VARS):
-            value = resid[b, i] - apply(side, b, i, (west, east))
+            value = resid[b, i] - sided[b, i]
+            acc = None
+            for j in range(VARS):
+                at = b * PAIR + (i * VARS + j) * SLOTS
+                term = jnp.where(lane == 0, row(side, at), row(side, at + 1)) * edge[j]
+                acc = term if acc is None else acc + term
+            value = value - acc
             resid[b, i] = value
             square = square + value * value
         return square
 
-    square = lax.fori_loop(0, blocks, side_part, none)
+    def edge_parts(n, square):
+        for m in range(UNROLL):
+            square = edge_part(n * UNROLL + m, square)
+        return square
+
+    square = lax.fori_loop(0, blocks // UNROLL, edge_parts, none)
     store_resid = pltpu.make_async_copy(resid, resid_out, out_sem.at[1])
     store_resid.start()
     sums = jnp.sum(square, axis=1, keepdims=True)
@@ -487,14 +513,30 @@
         remote(dst.at[rows], dst.at[rows], 8 + n, peer(1)).wait_send()
 
 
-def scale_kernel(entries, corr, resid, total, corr_out, out):
+def scale_kernel(entries, corr, resid, total, corr_out, out, held, piece, sums_in, load_sem, store_sem):
+    parts = piece.shape[0] // 8
+    rows = [pl.ds(8 * n, 8) for n in range(parts)]
+    loads = [pltpu.make_async_copy(total, sums_in, load_sem.at[parts])]
+    loads += [pltpu.make_async_copy(resid.at[r], piece.at[r], load_sem.at[n]) for n, r in enumerate(rows)]
+    loads += [pltpu.make_async_copy(corr, held, load_sem.at[parts + 1])]
+    stores = [pltpu.make_async_copy(piece.at[r], out.at[r], store_sem.at[n]) for n, r in enumerate(rows)]
+    stores += [pltpu.make_async_copy(held, corr_out, store_sem.at[parts])]
+    for load in loads:
+        load.start()
     lane = lanes_of((RHS, LANES))
     diagonal = lax.broadcasted_iota(jnp.int32, (RHS, LANES), 0) == lane
-    wide = jnp.broadcast_to(total[...], (RHS, LANES))
+    loads[0].wait()
+    wide = jnp.broadcast_to(sums_in[...], (RHS, LANES))
     sums = jnp.sum(jnp.where(diagonal, wide, 0.0), axis=1, keepdims=True)
     factor = jnp.broadcast_to(lax.rsqrt(sums / entries + 1e-6), (RHS, LANES))
-    out[...] = resid[...] * factor[None, None]
-    corr_out[...] = corr[...]
+    for n, r in enumerate(rows):
+        loads[1 + n].wait()
+        piece[r] = piece[r] * factor[None, None]
+        stores[n].start()
+    loads[-1].wait()
+    stores[-1].start()
+    for store in stores:
+        store.wait()
 
 
 def spec(space):
@@ -518,9 +560,10 @@
     corr, resid, total = pl.pallas_call(
         functools.partial(main_kernel, nodes, subs, line),
         out_shape=(plane, plane, jax.ShapeDtypeStruct((1, cells), F32)),
-        in_specs=[spec(pltpu.SMEM)] * 3 + [spec(pl.ANY)] * 5,
+        in_specs=[spec(pl.ANY)] * 8,
         out_specs=(spec(pl.ANY), spec(pl.ANY), spec(VMEM)),
-        scratch_shapes=[VMEM(plane.shape, F32)]
+        scratch_shapes=[pltpu.SMEM((SLOTS, blocks), jnp.int32)] * 3
+        + [VMEM(plane.shape, F32)] * 2
         + [VMEM(x.shape, F32) for x in (rhs, dinv, low, up, side)]
         + [VMEM((PAIR, blocks, cells), F32)] * 2
         + [VMEM((padded, VARS, wide, cells), F32) for wide in (FWIDE, GWIDE, FWIDE)]
@@ -529,23 +572,25 @@
         + [VMEM((depth, STATE, GWIDE, cells), F32)] * 2
         + [window] * 2
         + [VMEM((REACH, VARS, RHS, cells), F32)]
+        + [VMEM((RHS * LANES, cells), F32)]
         + [VMEM((2, RHS, cells), F32)] * 2
         + [VMEM((1, cells), F32)] * 2
         + [VMEM((line, 1, cells), F32), VMEM((across, 1, cells), F32)]
-        + [pltpu.SemaphoreType.DMA((n,)) for n in (5, 10, 10, 7, 2)],
+        + [pltpu.SemaphoreType.DMA((n,)) for n in (8, 10, 10, 7, 2)],
         compiler_params=pltpu.CompilerParams(
             collective_id=0, has_side_effects=True, vmem_limit_bytes=VMEM_LIMIT
         ),
         name="sweeps",
     )(lower_cols.T, upper_cols.T, counts.T, rhs, dinv, low, up, side)
-    slab = pl.BlockSpec((8, VARS, RHS, cells), lambda n: (n, 0, 0, 0))
     entries = nodes * blocks * VARS * subs * cells
     return pl.pallas_call(
         functools.partial(scale_kernel, entries),
         out_shape=(plane, plane),
-        grid=(blocks // 8,),
-        in_specs=[slab, slab, pl.BlockSpec((1, cells), lambda n: (0, 0))],
-        out_specs=(slab, slab),
+        in_specs=[spec(pl.ANY)] * 3,
+        out_specs=(spec(pl.ANY),) * 2,
+        scratch_shapes=[VMEM(plane.shape, F32)] * 2
+        + [VMEM((1, cells), F32)]
+        + [pltpu.SemaphoreType.DMA((blocks // 8 + n,)) for n in (2, 1)],
         compiler_params=pltpu.CompilerParams(vmem_limit_bytes=VMEM_LIMIT),
         name="scale",
     )(corr, resid, total)

time: 57.4 us -> 53.1 us (0.925)
  Pallas kernels: 56.7 us -> 52.3 us
    pallas_call x1, Pallas kernels: 53.6 us -> 50.2 us  [shards(): pl.pallas_call(functools.partial(main_kernel, nodes, subs, line), out_sha...]
    pallas_call x1, Pallas kernels: 3.08 us -> 2.14 us  [shards(): pl.pallas_call(functools.partial(scale_kernel, entries), out_shape=(plane...]
where the time goes in v3:
time: 53.1 us; the launch traced here: 52.9 us
  Pallas kernels  52.3 us (98%)
  between operations  0.64 us (1%)
    pallas_call x1, Pallas kernels, shards(): pl.pallas_call(functools.partial(main_kernel, nodes, subs, line), out_sha...  50.2 us
    pallas_call x1, Pallas kernels, shards(): pl.pallas_call(functools.partial(scale_kernel, entries), out_shape=(plane...  2.14 us

profile of v3, /device:TPU:1, one launch (start us, length us, event | category | flops | bytes accessed | tf_op | source)
XLA Modules:
  0.0 52.9 jit_solution(6476210310741842415)
XLA Ops:
  0.6 50.2 %sweeps.1 = (f32[24,5,8,128]{3,2,1,0:T(8,128)}, f32[24,5,8,128]{3,2,1,0:T(8,128)}, f32[1,128]{1,0:T(1,128)}) custom-call(s32[2,24]{1,0:T(2,128)} %bitcast.19, s32[2,24]{1,0:T(2,128)} %bitcast.20, s32[2,24]{1,0:T(2,128)} %bitcast.21, f32[24,5,8,128]{3,2,1,0:T(8,128)} %rhs_in.1, f32[25,24,128]{2,1,0:T(8,128)} %bitcast.18, f32[1200,128]{1,0:T(8,128)} %bitcast.15, ...), custom_call_target="tpu_custom_call" | custom-call | tf_op jit(solution)/shard_map/sweeps/pallas_call | solution.py:560
  50.8 2.1 %scale.1 = (f32[24,5,8,128]{3,2,1,0:T(8,128)}, f32[24,5,8,128]{3,2,1,0:T(8,128)}) custom-call(f32[24,5,8,128]{3,2,1,0:T(8,128)} %get-tuple-element.5.corr, f32[24,5,8,128]{3,2,1,0:T(8,128)} %get-tuple-element.6.resid, f32[1,128]{1,0:T(1,128)} %get-tuple-element.7.total), custom_call_target="tpu_custom_call" | custom-call | tf_op jit(solution)/shard_map/scale/pallas_call | solution.py:586

commit v4 on v3

--- a/solution.py
+++ b/solution.py
@@ -75,21 +75,31 @@
             emit(i, t, p + q)
 
 
-def pack(vals, tiles, send):
-    half = LANES // 2
+def pack(vals, tiles, send, span):
     for tile in range(tiles):
         turned = vals[tile * LANES : (tile + 1) * LANES, :].T
         for c in range(2):
-            for first in range(0, half, 8):
+            for first in range(0, span, 8):
                 at = first * SLOT + c * tiles + tile
-                send[pl.ds(at, 8, stride=SLOT), :] = turned[c * half + first : c * half + first + 8]
-
-
-def unpack(recv, tiles, vals):
-    half = LANES // 2
+                send[pl.ds(at, 8, stride=SLOT), :] = turned[c * span + first : c * span + first + 8]
+
+
+def unpack(recv, tiles, vals, span):
     for tile in range(tiles):
-        both = [recv[pl.ds(c * tiles + tile, half, stride=SLOT), :] for c in range(2)]
+        both = [recv[pl.ds(c * tiles + tile, span, stride=SLOT), :] for c in range(2)]
+        both = both * (LANES // (2 * span))
         vals[tile * LANES : (tile + 1) * LANES, :] = jnp.concatenate(both, 0).T
+
+
+def times(coef, values, start):
+    out = []
+    for i in range(STATE):
+        acc = list(start(i))
+        for j in range(STATE):
+            c = coef(i, j)
+            acc = [c * x if a is None else a + c * x for a, x in zip(acc, values[j])]
+        out.append(acc)
+    return out
 
 
 def shifts(span):
@@ -132,7 +142,7 @@
     nodes, subs, line, lcol_in, ucol_in, counts_in, rhs_in, dinv_in, low_in, up_in, side_in,
     corr_out, resid_out, total,
     lcol, ucol, counts, resid, sided, rhs, dinv, low, up, side, alow, aup, y, zb, zm, vals,
-    s1, s2, s3, r1, r2, r3, s4, s5, r4, r5, gf, gb,
+    s1, s2, s3, r4, r5, r1, r2, r3, s4, s5, gf, gb, yp, zbp, zmp, mid, enters, follows,
     zpad, upad, before, outer, edges, beside, part, stage, wide, deep,
     load_sem, send_sem, recv_sem, own_sem, out_sem,
 ):
@@ -186,31 +196,48 @@
             device_id_type=MESH,
         )
 
-    mine = pl.multiple_of(me * SLOT, SLOT)
-
-    def own(src, dst, tiles, n):
-        rows = pl.ds(mine, 2 * tiles)
-        return pltpu.make_async_copy(src.at[rows], dst.at[rows], own_sem.at[n])
-
-    def post(src, dst, tiles, n):
-        own(src, dst, tiles, n).start()
+    chips, chip, core = nodes // 2, me // 2, lax.rem(me, 2)
+
+    def slot(n, tiles):
+        return pl.ds(pl.multiple_of(n * SLOT, SLOT), 2 * tiles)
+
+    def own(src, dst, tiles, n, out, inside):
+        return pltpu.make_async_copy(src.at[slot(out, tiles)], dst.at[slot(inside, tiles)], own_sem.at[n])
+
+    def post(src, dst, tiles, n, out, inside):
+        own(src, dst, tiles, n, out(me), inside).start()
 
         def one(k, carry):
             to = lax.rem(me + k, nodes)
-            there = pl.ds(pl.multiple_of(to * SLOT, SLOT), 2 * tiles)
-            remote(src.at[there], dst.at[pl.ds(mine, 2 * tiles)], n, {"chain": to}).start()
+            remote(src.at[slot(out(to), tiles)], dst.at[slot(inside, tiles)], n, {"chain": to}).start()
             return carry
 
         for low_k, high_k in spans:
             lax.fori_loop(low_k, high_k, one, 0)
 
-    def whole(src, dst, tiles, n):
-        rows = pl.ds(0, 2 * tiles * (nodes - 1))
-        return remote(src.at[rows], dst.at[rows], n, around(1))
-
-    def collect(src, dst, tiles, n):
-        own(src, dst, tiles, n).wait()
-        whole(src, dst, tiles, n).wait_recv()
+    def whole(ref, tiles, n, count):
+        rows = pl.ds(0, 2 * tiles * count)
+        return remote(ref.at[rows], ref.at[rows], n, around(1))
+
+    def post_map(src, dst, tiles, n):
+        post(src, dst, tiles, n, lambda to: to, chip)
+
+    def post_state(src, dst, n):
+        post(src, dst, ONE, n, lambda to: to // 2, me)
+
+    def collect_map(src, dst, tiles, n, sender):
+        @pl.when(core == sender)
+        def _():
+            own(src, dst, tiles, n, me, chip).wait()
+            whole(dst, tiles, n, chips - 1).wait_recv()
+
+        @pl.when(core != sender)
+        def _():
+            whole(dst, tiles, n, chips).wait_recv()
+
+    def collect_state(src, dst, n):
+        own(src, dst, ONE, n, chip, me).wait()
+        whole(dst, ONE, n, nodes - 1).wait_recv()
 
     fsub = lax.broadcasted_iota(jnp.int32, (FWIDE, LANES), 0)
     gsub = lax.broadcasted_iota(jnp.int32, (GWIDE, LANES), 0)
@@ -263,11 +290,7 @@
         return carry
 
     lax.fori_loop(0, blocks, forward, 0)
-    for d in range(1, REACH + 1):
-        for v in range(VARS):
-            q = (d - 1) * VARS + v
-            vals[q * FWIDE : (q + 1) * FWIDE, :] = y[REACH + blocks - d, v]
-    pack(vals, FULL, s1)
+
     loads[3].wait()
     couple(up, dinv, aup, blocks)
 
@@ -281,11 +304,7 @@
         return carry
 
     lax.fori_loop(0, blocks, basis, 0)
-    for d in range(1, REACH + 1):
-        for v in range(VARS):
-            q = (d - 1) * VARS + v
-            vals[q * GWIDE : (q + 1) * GWIDE, :] = zb[d - 1, v]
-    pack(vals, MAP, s2)
+
     def backward(step, carry):
         b = blocks - 1 - step
 
@@ -296,55 +315,151 @@
         return carry
 
     lax.fori_loop(0, blocks, backward, 0)
-    for d in range(1, REACH + 1):
-        for v in range(VARS):
-            q = (d - 1) * VARS + v
-            vals[q * FWIDE : (q + 1) * FWIDE, :] = zm[d - 1, v]
-    pack(vals, FULL, s3)
     pl.semaphore_wait(barrier, nodes + across - 2)
-    post(s1, r1, FULL, 0)
-    post(s2, r2, MAP, 1)
-    post(s3, r3, FULL, 2)
+
+    partner = {"chain": me + 1 - 2 * core}
+    ends = (y.at[pl.ds(blocks, REACH)], zb.at[pl.ds(0, REACH)], zm.at[pl.ds(0, REACH)])
+    pairs = [
+        remote(src, dst, 10 + n, partner) for n, (src, dst) in enumerate(zip(ends, (yp, zbp, zmp)))
+    ]
+    for copy in pairs:
+        copy.start()
+
+    def at_state(q):
+        return q // VARS, q % VARS
+
+    def forward_at(ref, last):
+        def index(q):
+            d, v = at_state(q)
+            return ref, last - d, v
+
+        return index
+
+    def backward_at(ref):
+        def index(q):
+            d, v = at_state(q)
+            return ref, d, v
+
+        return index
+
+    def chunks(index, span):
+        parts = []
+        for q in range(STATE):
+            ref, d, v = index(q)
+            parts.append([ref[d, v, chunk(t), :] for t in span])
+        return parts
+
+    def entry(index, offset):
+        def coef(i, j):
+            ref, d, v = index(i)
+            return row(ref, d, v, offset + j)
+
+        return coef
+
+    mine_f, mine_b, mine_m = forward_at(y, blocks + REACH - 1), backward_at(zb), backward_at(zm)
+    other_f, other_b, other_m = forward_at(yp, REACH - 1), backward_at(zbp), backward_at(zmp)
+
+    def put(out, wide, parts):
+        for i, part in enumerate(parts):
+            for t, value in enumerate(part):
+                out[i * wide + 8 * t : i * wide + 8 * t + 8, :] = value
+
+    pairs[0].wait_recv()
+
+    @pl.when(core == 0)
+    def _():
+        heads = chunks(other_f, (0,))
+        for t in range(3):
+            values = chunks(mine_f, (t,))
+            start_of = (lambda i: heads[i]) if t == 0 else (lambda i: [None])
+            for i, (value,) in enumerate(times(entry(other_f, RHS), values, start_of)):
+                vals[i * FWIDE + 8 * t : i * FWIDE + 8 * t + 8, :] = value
+        pack(vals, FULL, s1, nodes)
+        post_map(s1, r1, FULL, 0)
+        pairs[1].wait_recv()
+        values = chunks(other_b, (0, 1))
+        put(vals, GWIDE, times(entry(mine_b, 0), values, lambda i: [None, None]))
+        pack(vals, MAP, s2, nodes)
+        post_map(s2, r2, MAP, 1)
+        pairs[2].wait_recv()
+
+    @pl.when(core == 1)
+    def _():
+        heads = chunks(mine_m, (0,))
+        for t in range(3):
+            values = chunks(other_f, (t,))
+            start_of = (lambda i: heads[i]) if t == 0 else (lambda i: [None])
+            for i, (value,) in enumerate(times(entry(mine_m, RHS), values, start_of)):
+                mid[i, chunk(t), :] = value
+        pairs[1].wait_recv()
+        pairs[2].wait_recv()
+        for t in range(3):
+            values = [[mid[j, chunk(t), :]] for j in range(STATE)]
+            heads = chunks(other_m, (t,))
+            for i, (value,) in enumerate(times(entry(other_b, 0), values, lambda i: heads[i])):
+                vals[i * FWIDE + 8 * t : i * FWIDE + 8 * t + 8, :] = value
+        pack(vals, FULL, s3, nodes)
+        post_map(s3, r3, FULL, 2)
 
     lane = lanes_of((RHS, LANES))
-    at = lax.rem(lane, nodes)
-    collect(s1, r1, FULL, 0)
-    unpack(r1, FULL, vals)
+    at = lax.rem(lane, chips)
+    collect_map(s1, r1, FULL, 0, 0)
+    unpack(r1, FULL, vals, chips)
     for i in range(STATE):
         gf[0, i] = vals[i * FWIDE + RHS : (i + 1) * FWIDE, :]
-    scan_maps(gf, at, nodes, False)
+    scan_maps(gf, at, chips, False)
     entering = scan_states(
-        gf, [vals[i * FWIDE : i * FWIDE + RHS, :] for i in range(STATE)], at, nodes, False
+        gf, [vals[i * FWIDE : i * FWIDE + RHS, :] for i in range(STATE)], at, chips, False
     )
     vals[STATE * RHS : LANES, :] = none
     for i in range(STATE):
         vals[i * RHS : (i + 1) * RHS, :] = entering[i]
-    pack(vals, ONE, s4)
-    post(s4, r4, ONE, 3)
-
-    collect(s2, r2, MAP, 1)
-    unpack(r2, MAP, vals)
+    pack(vals, ONE, s4, chips)
+    post_state(s4, r4, 3)
+
+    collect_map(s2, r2, MAP, 1, 0)
+    unpack(r2, MAP, vals, chips)
     for i in range(STATE):
         gb[0, i] = vals[i * GWIDE : (i + 1) * GWIDE, :]
-    scan_maps(gb, at, nodes, True)
-    collect(s3, r3, FULL, 2)
-    unpack(r3, FULL, vals)
+    scan_maps(gb, at, chips, True)
+    collect_map(s3, r3, FULL, 2, 1)
+    unpack(r3, FULL, vals, chips)
     state = []
     for i in range(STATE):
         acc = vals[i * FWIDE : i * FWIDE + RHS, :]
         for j in range(STATE):
             acc = acc + row(vals, i * FWIDE + RHS + j) * entering[j]
         state.append(acc)
-    following = scan_states(gb, state, at, nodes, True)
+    following = scan_states(gb, state, at, chips, True)
     vals[STATE * RHS : LANES, :] = none
     for i in range(STATE):
         vals[i * RHS : (i + 1) * RHS, :] = following[i]
-    pack(vals, ONE, s5)
-    post(s5, r5, ONE, 4)
-
-    collect(s4, r4, ONE, 3)
-    unpack(r4, ONE, vals)
-    entering = [vals[i * RHS : (i + 1) * RHS, :] for i in range(STATE)]
+    pack(vals, ONE, s5, chips)
+    post_state(s5, r5, 4)
+
+    collect_state(s4, r4, 3)
+    unpack(r4, ONE, vals, nodes)
+
+    def states():
+        return [[vals[i * RHS : (i + 1) * RHS, :]] for i in range(STATE)]
+
+    @pl.when(core == 0)
+    def _():
+        heads = chunks(mine_f, (0,))
+        between = times(entry(mine_f, RHS), states(), lambda i: heads[i])
+        heads = chunks(other_m, (0,))
+        for i, (value,) in enumerate(times(entry(other_m, RHS), between, lambda i: heads[i])):
+            follows[i] = value
+        for i, (value,) in enumerate(states()):
+            enters[i] = value
+
+    @pl.when(core == 1)
+    def _():
+        heads = chunks(other_f, (0,))
+        for i, (value,) in enumerate(times(entry(other_f, RHS), states(), lambda i: heads[i])):
+            enters[i] = value
+
+    entering = [enters[i] for i in range(STATE)]
 
     def enter(b, carry):
         for i in range(VARS):
@@ -355,9 +470,22 @@
         return carry
 
     lax.fori_loop(0, blocks, enter, 0)
-    collect(s5, r5, ONE, 4)
-    unpack(r5, ONE, vals)
-    following = [vals[i * RHS : (i + 1) * RHS, :] for i in range(STATE)]
+    collect_state(s5, r5, 4)
+    unpack(r5, ONE, vals, nodes)
+
+    @pl.when(core == 0)
+    def _():
+        for i, (value,) in enumerate(
+            times(entry(other_b, 0), states(), lambda i: [follows[i]])
+        ):
+            follows[i] = value
+
+    @pl.when(core == 1)
+    def _():
+        for i, (value,) in enumerate(states()):
+            follows[i] = value
+
+    following = [follows[i] for i in range(STATE)]
     for d in range(1, REACH + 1):
         for v in range(VARS):
             zpad[blocks - 1 + d, v] = following[(d - 1) * VARS + v]
@@ -502,10 +630,20 @@
 
     store_corr.wait()
     store_resid.wait()
-    for src, dst, tiles, n in (
-        (s1, r1, FULL, 0), (s2, r2, MAP, 1), (s3, r3, FULL, 2), (s4, r4, ONE, 3), (s5, r5, ONE, 4)
-    ):
-        whole(src, dst, tiles, n).wait_send()
+
+    @pl.when(core == 0)
+    def _():
+        whole(s1, FULL, 0, nodes - 1).wait_send()
+        whole(s2, MAP, 1, nodes - 1).wait_send()
+
+    @pl.when(core == 1)
+    def _():
+        whole(s3, FULL, 2, nodes - 1).wait_send()
+
+    for n, ref in ((3, r4), (4, r5)):
+        whole(ref, ONE, n, nodes - 1).wait_send()
+    for copy in pairs:
+        copy.wait_send()
     for copy in halo:
         copy.wait_send()
     for n, (peer, count, _, _, dst, _) in enumerate(rounds):
@@ -556,7 +694,8 @@
     plane = jax.ShapeDtypeStruct((blocks, VARS, RHS, cells), F32)
     slots = VMEM((nodes * SLOT, cells), F32)
     window = VMEM((padded, VARS, RHS, cells), F32)
-    depth = len(shifts(nodes))
+    half_slots = VMEM((nodes // 2 * SLOT, cells), F32)
+    depth = len(shifts(nodes // 2))
     corr, resid, total = pl.pallas_call(
         functools.partial(main_kernel, nodes, subs, line),
         out_shape=(plane, plane, jax.ShapeDtypeStruct((1, cells), F32)),
@@ -568,15 +707,18 @@
         + [VMEM((PAIR, blocks, cells), F32)] * 2
         + [VMEM((padded, VARS, wide, cells), F32) for wide in (FWIDE, GWIDE, FWIDE)]
         + [VMEM((FULL * LANES, cells), F32)]
-        + [slots] * 10
+        + [slots] * 5
+        + [half_slots] * 5
         + [VMEM((depth, STATE, GWIDE, cells), F32)] * 2
+        + [VMEM((REACH, VARS, wide, cells), F32) for wide in (FWIDE, GWIDE, FWIDE)]
+        + [VMEM((STATE, wide, cells), F32) for wide in (FWIDE, RHS, RHS)]
         + [window] * 2
         + [VMEM((REACH, VARS, RHS, cells), F32)]
         + [VMEM((RHS * LANES, cells), F32)]
         + [VMEM((2, RHS, cells), F32)] * 2
         + [VMEM((1, cells), F32)] * 2
         + [VMEM((line, 1, cells), F32), VMEM((across, 1, cells), F32)]
-        + [pltpu.SemaphoreType.DMA((n,)) for n in (8, 10, 10, 7, 2)],
+        + [pltpu.SemaphoreType.DMA((n,)) for n in (8, 13, 13, 7, 2)],
         compiler_params=pltpu.CompilerParams(
             collective_id=0, has_side_effects=True, vmem_limit_bytes=VMEM_LIMIT
         ),

time: 53.1 us -> 49.5 us (0.932)
  Pallas kernels: 52.3 us -> 48.8 us
    pallas_call x1, Pallas kernels: 50.2 us -> 46.6 us  [shards(): pl.pallas_call(functools.partial(main_kernel, nodes, subs, line), out_sha...]
where the time goes in v4:
time: 49.5 us; the launch traced here: 49.4 us
  Pallas kernels  48.8 us (99%)
  between operations  0.64 us (1%)
    pallas_call x1, Pallas kernels, shards(): pl.pallas_call(functools.partial(main_kernel, nodes, subs, line), out_sha...  46.6 us
    pallas_call x1, Pallas kernels, shards(): pl.pallas_call(functools.partial(scale_kernel, entries), out_shape=(plane...  2.14 us

profile of v4, /device:TPU:1, one launch (start us, length us, event | category | flops | bytes accessed | tf_op | source)
XLA Modules:
  0.0 49.4 jit_solution(7130525181261263405)
XLA Ops:
  0.6 46.6 %sweeps.1 = (f32[24,5,8,128]{3,2,1,0:T(8,128)}, f32[24,5,8,128]{3,2,1,0:T(8,128)}, f32[1,128]{1,0:T(1,128)}) custom-call(s32[2,24]{1,0:T(2,128)} %bitcast.19, s32[2,24]{1,0:T(2,128)} %bitcast.20, s32[2,24]{1,0:T(2,128)} %bitcast.21, f32[24,5,8,128]{3,2,1,0:T(8,128)} %rhs_in.1, f32[25,24,128]{2,1,0:T(8,128)} %bitcast.18, f32[1200,128]{1,0:T(8,128)} %bitcast.15, ...), custom_call_target="tpu_custom_call" | custom-call | tf_op jit(solution)/shard_map/sweeps/pallas_call | solution.py:699
  47.3 2.1 %scale.1 = (f32[24,5,8,128]{3,2,1,0:T(8,128)}, f32[24,5,8,128]{3,2,1,0:T(8,128)}) custom-call(f32[24,5,8,128]{3,2,1,0:T(8,128)} %get-tuple-element.5.corr, f32[24,5,8,128]{3,2,1,0:T(8,128)} %get-tuple-element.6.resid, f32[1,128]{1,0:T(1,128)} %get-tuple-element.7.total), custom_call_target="tpu_custom_call" | custom-call | tf_op jit(solution)/shard_map/scale/pallas_call | solution.py:728

commit v5 on v4

--- a/solution.py
+++ b/solution.py
@@ -82,6 +82,18 @@
             for first in range(0, span, 8):
                 at = first * SLOT + c * tiles + tile
                 send[pl.ds(at, 8, stride=SLOT), :] = turned[c * span + first : c * span + first + 8]
+
+
+def each(low, high, step):
+    count = high - low
+    some = next(n for n in (8, 5, 4, 3, 1) if count % n == 0)
+
+    def trip(n, carry):
+        for m in range(some):
+            step(low + n * some + m)
+        return carry
+
+    lax.fori_loop(0, count // some, trip, 0)
 
 
 def unpack(recv, tiles, vals, span):
@@ -180,11 +192,10 @@
     for peer, spans_of in ((around, spans[:1]), (cross, ((1, across),)), (around, spans[1:])):
         for low_k, high_k in spans_of:
 
-            def greet(k, carry, peer=peer):
+            def greet(k, peer=peer):
                 pl.semaphore_signal(barrier, inc=1, device_id=peer(k), device_id_type=MESH)
-                return carry
-
-            lax.fori_loop(low_k, high_k, greet, 0)
+
+            each(low_k, high_k, greet)
 
     def remote(src, dst, n, peer):
         return pltpu.make_async_remote_copy(
@@ -207,13 +218,12 @@
     def post(src, dst, tiles, n, out, inside):
         own(src, dst, tiles, n, out(me), inside).start()
 
-        def one(k, carry):
+        def one(k):
             to = lax.rem(me + k, nodes)
             remote(src.at[slot(out(to), tiles)], dst.at[slot(inside, tiles)], n, {"chain": to}).start()
-            return carry
 
         for low_k, high_k in spans:
-            lax.fori_loop(low_k, high_k, one, 0)
+            each(low_k, high_k, one)
 
     def whole(ref, tiles, n, count):
         rows = pl.ds(0, 2 * tiles * count)
@@ -271,9 +281,11 @@
     for n in (5, 6, 7, 0, 1):
         loads[n].wait()
     couple(low, dinv, alow, blocks)
+    loads[3].wait()
+    couple(up, dinv, aup, blocks)
     loads[2].wait()
 
-    def forward(b, carry):
+    def forward(b):
         values = window(y, lower(b), 3)
         src = [rhs[b, m] for m in range(VARS)]
         own_part = []
@@ -287,23 +299,20 @@
             y[b + REACH, i, chunk(t), :] = own_part[i] - value if t == 0 else -value
 
         coupled(alow, b, values, emit)
-        return carry
-
-    lax.fori_loop(0, blocks, forward, 0)
-
-    loads[3].wait()
-    couple(up, dinv, aup, blocks)
-
-    def basis(step, carry):
-        b = blocks - 1 - step
+
+    def basis(b):
 
         def emit(i, t, value):
             zb[b, i, chunk(t), :] = -value
 
         coupled(aup, b, window(zb, upper(b), 2), emit)
+
+    def both_ways(b, carry):
+        forward(b)
+        basis(blocks - 1 - b)
         return carry
 
-    lax.fori_loop(0, blocks, basis, 0)
+    lax.fori_loop(0, blocks, both_ways, 0)
 
     def backward(step, carry):
         b = blocks - 1 - step
@@ -490,15 +499,14 @@
         for v in range(VARS):
             zpad[blocks - 1 + d, v] = following[(d - 1) * VARS + v]
 
-    def follow(b, carry):
+    def follow(b):
         for i in range(VARS):
             acc = zpad[b, i]
             for j in range(STATE):
                 acc = acc + row(zb, b, i, j) * following[j]
             zpad[b, i] = acc
-        return carry
-
-    lax.fori_loop(0, blocks, follow, 0)
+
+    each(0, blocks, follow)
     rows_of = zpad.reshape(zpad.shape[0] * VARS * RHS, LANES)
     for tile in range(RHS):
         columns = rows_of[tile * LANES : (tile + 1) * LANES, :].T
@@ -512,11 +520,8 @@
     ]
     halo[0].start()
     halo[1].start()
-    store_corr = pltpu.make_async_copy(zpad.at[pl.ds(0, blocks)], corr_out, out_sem.at[0])
-    store_corr.start()
-
-    def difference(step, carry):
-        b = blocks - 1 - step
+
+    def difference(b):
 
         def emit(i, t, value):
             upad[b + REACH, i] = value
@@ -524,11 +529,12 @@
         at = upper(b)
         values = [[[zpad[at[k], j]] for j in range(VARS)] for k in range(SLOTS)]
         coupled(aup, b, values, emit)
-        return carry
-
-    lax.fori_loop(0, REACH, difference, 0)
+
+    each(blocks - REACH, blocks, difference)
     halo[2].start()
-    lax.fori_loop(REACH, blocks, difference, 0)
+    store_corr = pltpu.make_async_copy(zpad.at[pl.ds(0, blocks)], corr_out, out_sem.at[0])
+    store_corr.start()
+    each(0, blocks - REACH, difference)
 
     def apply(coef, b, i, values):
         total = None
@@ -540,17 +546,15 @@
             total = acc if total is None else total + acc
         return total
 
-    def before_part(b, carry):
+    def before_part(b):
         at = lower(b)
         values = [[upad[at[k], j] for j in range(VARS)] for k in range(SLOTS)]
         for i in range(VARS):
             resid[b, i] = apply(low, b, i, values)
-        return carry
-
-    lax.fori_loop(REACH, blocks, before_part, 0)
+
     loads[4].wait()
 
-    def inner_part(b, carry):
+    def inner_part(b):
         west, east = [], []
         for j in range(VARS):
             value = zpad[b, j]
@@ -558,19 +562,18 @@
             east.append(jnp.where(lane == LANES - 1, 0.0, pltpu.roll(value, LANES - 1, 1)))
         for i in range(VARS):
             sided[b, i] = apply(side, b, i, (west, east))
-        return carry
-
-    def inner_parts(n, carry):
-        for m in range(UNROLL):
-            inner_part(n * UNROLL + m, carry)
-        return carry
-
-    lax.fori_loop(0, blocks // UNROLL, inner_parts, 0)
+
+    def inside(b):
+        before_part(b)
+        inner_part(b)
+
+    each(REACH, blocks, inside)
+    each(0, REACH, inner_part)
     halo[2].wait_recv()
     for d in range(REACH):
         for v in range(VARS):
             upad[d, v] = jnp.where(me == 0, 0.0, before[d, v])
-    lax.fori_loop(0, REACH, before_part, 0)
+    each(0, REACH, before_part)
     halo[0].wait_recv()
     halo[1].wait_recv()
     whole_row = (LANES, LANES)
@@ -616,11 +619,10 @@
     rounds = ((along, line, place, part, wide, stage), (cross, across, flat, stage, deep, total))
     for n, (peer, count, index, src, dst, out) in enumerate(rounds):
 
-        def tell(k, carry, peer=peer, src=src, dst=dst, index=index, n=n):
+        def tell(k, peer=peer, src=src, dst=dst, index=index, n=n):
             remote(src, dst.at[index], 8 + n, peer(k)).start()
-            return carry
-
-        lax.fori_loop(1, count, tell, 0)
+
+        each(1, count, tell)
         mine_too = pltpu.make_async_copy(src, dst.at[index], own_sem.at[5 + n])
         mine_too.start()
         mine_too.wait()

time: 49.5 us -> 48.7 us (0.984)
  Pallas kernels: 48.8 us -> 47.9 us
    pallas_call x1, Pallas kernels: 46.6 us -> 45.8 us  [shards(): pl.pallas_call(functools.partial(main_kernel, nodes, subs, line), out_sha...]
where the time goes in v5:
time: 48.7 us; the launch traced here: 48.6 us
  Pallas kernels  47.9 us (98%)
  between operations  0.64 us (1%)
    pallas_call x1, Pallas kernels, shards(): pl.pallas_call(functools.partial(main_kernel, nodes, subs, line), out_sha...  45.8 us
    pallas_call x1, Pallas kernels, shards(): pl.pallas_call(functools.partial(scale_kernel, entries), out_shape=(plane...  2.14 us

profile of v5, /device:TPU:1, one launch (start us, length us, event | category | flops | bytes accessed | tf_op | source)
XLA Modules:
  0.0 48.6 jit_solution(13801250828848736215)
XLA Ops:
  0.6 45.8 %sweeps.1 = (f32[24,5,8,128]{3,2,1,0:T(8,128)}, f32[24,5,8,128]{3,2,1,0:T(8,128)}, f32[1,128]{1,0:T(1,128)}) custom-call(s32[2,24]{1,0:T(2,128)} %bitcast.19, s32[2,24]{1,0:T(2,128)} %bitcast.20, s32[2,24]{1,0:T(2,128)} %bitcast.21, f32[24,5,8,128]{3,2,1,0:T(8,128)} %rhs_in.1, f32[25,24,128]{2,1,0:T(8,128)} %bitcast.18, f32[1200,128]{1,0:T(8,128)} %bitcast.15, ...), custom_call_target="tpu_custom_call" | custom-call | tf_op jit(solution)/shard_map/sweeps/pallas_call | solution.py:701
  46.4 2.1 %scale.1 = (f32[24,5,8,128]{3,2,1,0:T(8,128)}, f32[24,5,8,128]{3,2,1,0:T(8,128)}) custom-call(f32[24,5,8,128]{3,2,1,0:T(8,128)} %get-tuple-element.5.corr, f32[24,5,8,128]{3,2,1,0:T(8,128)} %get-tuple-element.6.resid, f32[1,128]{1,0:T(1,128)} %get-tuple-element.7.total), custom_call_target="tpu_custom_call" | custom-call | tf_op jit(solution)/shard_map/scale/pallas_call | solution.py:730

commit v6 on v5

--- a/solution.py
+++ b/solution.py
@@ -152,8 +152,8 @@
 
 def main_kernel(
     nodes, subs, line, lcol_in, ucol_in, counts_in, rhs_in, dinv_in, low_in, up_in, side_in,
-    corr_out, resid_out, total,
-    lcol, ucol, counts, resid, sided, rhs, dinv, low, up, side, alow, aup, y, zb, zm, vals,
+    corr_out, resid, total,
+    lcol, ucol, counts, sided, rhs, dinv, low, up, side, alow, aup, y, zb, zm, vals,
     s1, s2, s3, r4, r5, r1, r2, r3, s4, s5, gf, gb, yp, zbp, zmp, mid, enters, follows,
     zpad, upad, before, outer, edges, beside, part, stage, wide, deep,
     load_sem, send_sem, recv_sem, own_sem, out_sem,
@@ -610,8 +610,6 @@
         return square
 
     square = lax.fori_loop(0, blocks // UNROLL, edge_parts, none)
-    store_resid = pltpu.make_async_copy(resid, resid_out, out_sem.at[1])
-    store_resid.start()
     sums = jnp.sum(square, axis=1, keepdims=True)
     diagonal = lax.broadcasted_iota(jnp.int32, (RHS, LANES), 0) == lane
     part[...] = jnp.sum(jnp.where(diagonal, sums, 0.0), axis=0, keepdims=True)
@@ -631,7 +629,6 @@
         out[...] = jnp.sum(dst[...], axis=0)
 
     store_corr.wait()
-    store_resid.wait()
 
     @pl.when(core == 0)
     def _():
@@ -653,28 +650,20 @@
         remote(dst.at[rows], dst.at[rows], 8 + n, peer(1)).wait_send()
 
 
-def scale_kernel(entries, corr, resid, total, corr_out, out, held, piece, sums_in, load_sem, store_sem):
-    parts = piece.shape[0] // 8
+def scale_kernel(entries, corr, resid, total, corr_out, out, scaled, store_sem):
+    parts = scaled.shape[0] // 8
     rows = [pl.ds(8 * n, 8) for n in range(parts)]
-    loads = [pltpu.make_async_copy(total, sums_in, load_sem.at[parts])]
-    loads += [pltpu.make_async_copy(resid.at[r], piece.at[r], load_sem.at[n]) for n, r in enumerate(rows)]
-    loads += [pltpu.make_async_copy(corr, held, load_sem.at[parts + 1])]
-    stores = [pltpu.make_async_copy(piece.at[r], out.at[r], store_sem.at[n]) for n, r in enumerate(rows)]
-    stores += [pltpu.make_async_copy(held, corr_out, store_sem.at[parts])]
-    for load in loads:
-        load.start()
+    stores = [pltpu.make_async_copy(scaled.at[r], out.at[r], store_sem.at[n]) for n, r in enumerate(rows)]
+    stores += [pltpu.make_async_copy(corr, corr_out, store_sem.at[parts])]
+    stores[-1].start()
     lane = lanes_of((RHS, LANES))
     diagonal = lax.broadcasted_iota(jnp.int32, (RHS, LANES), 0) == lane
-    loads[0].wait()
-    wide = jnp.broadcast_to(sums_in[...], (RHS, LANES))
+    wide = jnp.broadcast_to(total[...], (RHS, LANES))
     sums = jnp.sum(jnp.where(diagonal, wide, 0.0), axis=1, keepdims=True)
     factor = jnp.broadcast_to(lax.rsqrt(sums / entries + 1e-6), (RHS, LANES))
     for n, r in enumerate(rows):
-        loads[1 + n].wait()
-        piece[r] = piece[r] * factor[None, None]
+        scaled[r] = resid[r] * factor[None, None]
         stores[n].start()
-    loads[-1].wait()
-    stores[-1].start()
     for store in stores:
         store.wait()
 
@@ -700,11 +689,11 @@
     depth = len(shifts(nodes // 2))
     corr, resid, total = pl.pallas_call(
         functools.partial(main_kernel, nodes, subs, line),
-        out_shape=(plane, plane, jax.ShapeDtypeStruct((1, cells), F32)),
+        out_shape=(VMEM(plane.shape, F32), VMEM(plane.shape, F32), VMEM((1, cells), F32)),
         in_specs=[spec(pl.ANY)] * 8,
-        out_specs=(spec(pl.ANY), spec(pl.ANY), spec(VMEM)),
+        out_specs=(spec(VMEM),) * 3,
         scratch_shapes=[pltpu.SMEM((SLOTS, blocks), jnp.int32)] * 3
-        + [VMEM(plane.shape, F32)] * 2
+        + [VMEM(plane.shape, F32)]
         + [VMEM(x.shape, F32) for x in (rhs, dinv, low, up, side)]
         + [VMEM((PAIR, blocks, cells), F32)] * 2
         + [VMEM((padded, VARS, wide, cells), F32) for wide in (FWIDE, GWIDE, FWIDE)]
@@ -720,7 +709,7 @@
         + [VMEM((2, RHS, cells), F32)] * 2
         + [VMEM((1, cells), F32)] * 2
         + [VMEM((line, 1, cells), F32), VMEM((across, 1, cells), F32)]
-        + [pltpu.SemaphoreType.DMA((n,)) for n in (8, 13, 13, 7, 2)],
+        + [pltpu.SemaphoreType.DMA((n,)) for n in (8, 13, 13, 7, 1)],
         compiler_params=pltpu.CompilerParams(
             collective_id=0, has_side_effects=True, vmem_limit_bytes=VMEM_LIMIT
         ),
@@ -730,12 +719,10 @@
     return pl.pallas_call(
         functools.partial(scale_kernel, entries),
         out_shape=(plane, plane),
-        in_specs=[spec(pl.ANY)] * 3,
+        in_specs=[spec(VMEM)] * 3,
         out_specs=(spec(pl.ANY),) * 2,
-        scratch_shapes=[VMEM(plane.shape, F32)] * 2
-        + [VMEM((1, cells), F32)]
-        + [pltpu.SemaphoreType.DMA((blocks // 8 + n,)) for n in (2, 1)],
-        compiler_params=pltpu.CompilerParams(vmem_limit_bytes=VMEM_LIMIT),
+        scratch_shapes=[VMEM(plane.shape, F32), pltpu.SemaphoreType.DMA((blocks // 8 + 1,))],
+        compiler_params=pltpu.CompilerParams(vmem_limit_bytes=8 << 20),
         name="scale",
     )(corr, resid, total)
 

time: 48.7 us -> 47 us (0.965)
  Pallas kernels: 47.9 us -> 46.3 us
    pallas_call x1, Pallas kernels: 2.14 us -> 0.98 us  [shards(): pl.pallas_call(functools.partial(scale_kernel, entries), out_shape=(plane...]
    pallas_call x1, Pallas kernels: 45.8 us -> 45.3 us  [shards(): pl.pallas_call(functools.partial(main_kernel, nodes, subs, line), out_sha...]
where the time goes in v6:
time: 47 us; the launch traced here: 46.9 us
  Pallas kernels  46.3 us (99%)
  between operations  0.64 us (1%)
    pallas_call x1, Pallas kernels, shards(): pl.pallas_call(functools.partial(main_kernel, nodes, subs, line), out_sha...  45.3 us
    pallas_call x1, Pallas kernels, shards(): pl.pallas_call(functools.partial(scale_kernel, entries), out_shape=(plane...  0.98 us

profile of v6, /device:TPU:1, one launch (start us, length us, event | category | flops | bytes accessed | tf_op | source)
XLA Modules:
  0.0 46.9 jit_solution(15443158181304302129)
XLA Ops:
  0.6 45.3 %sweeps.1 = (f32[24,5,8,128]{3,2,1,0:T(8,128)S(1)}, f32[24,5,8,128]{3,2,1,0:T(8,128)S(1)}, f32[1,128]{1,0:T(1,128)S(1)}) custom-call(s32[2,24]{1,0:T(2,128)} %bitcast.19, s32[2,24]{1,0:T(2,128)} %bitcast.20, s32[2,24]{1,0:T(2,128)} %bitcast.21, f32[24,5,8,128]{3,2,1,0:T(8,128)} %rhs_in.1, f32[25,24,128]{2,1,0:T(8,128)} %bitcast.18, f32[1200,128]{1,0:T(8,128)} %bitcast.15, ...), custom_call_target="tpu_custom_call" | custom-call | tf_op jit(solution)/shard_map/sweeps/pallas_call | solution.py:690
  45.9 1.0 %scale.1 = (f32[24,5,8,128]{3,2,1,0:T(8,128)}, f32[24,5,8,128]{3,2,1,0:T(8,128)}) custom-call(f32[24,5,8,128]{3,2,1,0:T(8,128)S(1)} %get-tuple-element.5.corr, f32[24,5,8,128]{3,2,1,0:T(8,128)S(1)} %get-tuple-element.6.resid, f32[1,128]{1,0:T(1,128)S(1)} %get-tuple-element.7.total), custom_call_target="tpu_custom_call" | custom-call | tf_op jit(solution)/shard_map/scale/pallas_call | solution.py:719
